TPU v7x, 256 devices: a whole 4x4x8 slice. The times are simulated.
256 devices in a mesh: ang: 16 (over y_hi, x, core), row: 16 (over z, y_lo).
Axes of the slice: x: 4, y: 4 (y_hi: 2, y_lo: 2; y = y_hi * 2 + y_lo), z: 8, core: 2. Of those that a mesh axis runs over, the one named last changes fastest.
Arguments:
- dual_field: bfloat16 [64, 32, 2048], P('ang', 'row'), may hold values from -2 to 3
- forward: bfloat16 [64, 32, 2048], P('ang', 'row'), may hold values from -2 to 3
- sinogram: bfloat16 [64, 32, 2048], P('ang', 'row'), may hold values from -2 to 3
- first_weight: bfloat16 [3, 3, 32, 3], replicated, may hold values from -1.25 to 1.25
- first_bias: float32 [32], replicated, may hold values from -3 to 3
- middle_weight: bfloat16 [3, 3, 32, 32], replicated, may hold values from -0.375 to 0.375
- middle_bias: float32 [32], replicated, may hold values from -3 to 3
- last_weight: bfloat16 [3, 3, 1, 32], replicated, may hold values from -0.1875 to 0.1875
- magnify: float32 [64], P('ang'), may hold values from 0.85 to 0.95
- detector_shift: float32 [64], P('ang'), may hold values from -8 to 8
- row_fraction: float32 [64], P('ang'), may hold values from 0 to 1
- offsets: int32 [16, 64], replicated, may hold values from 0 to 27, as said below
- slab_order: int32 [64], replicated, may hold values from 0 to 63, each once
Outputs:
- new_dual: bfloat16 [64, 32, 2048], P('ang', 'row')
- volume: float32 [256, 2048], P('row', 'ang')
Inputs may be any that keep to these rules, and one draw needn't show every extreme that they name: offsets[b, q] lies within 2 rows of q * 27 // 63. `slab_order`: each slab appears once.
All inputs are finite; a program needn't handle non-finite values.
Results may differ from a plain program's by a relative error of at most 0.0022.
The roundings to bfloat16 on the way count: a program that leaves them out, or rounds other values in their place, can miss the bound.
Values may be sent and summed in bfloat16 or wider, within the bound.
No kernel may reach another device: no remote copies, remote signals or barrier semaphores. Data moves between devices by JAX's collectives and lax.ppermute only.
A program may use at most 64 MiB of HBM per device.

v0:
```python
import math

import jax
import jax.numpy as jnp
from jax import lax
from jax.sharding import PartitionSpec as P

SLAB_Z = 4
SLABS_DEV = 4


def extended(x, sides, width):
    for axis, dim in sides:
        count, length = (lax.axis_size(axis), x.shape[dim])
        up = [(i, (i + 1) % count) for i in range(count)]
        down = [(j, i) for i, j in up]
        last = lax.slice_in_dim(x, length - width, length, axis=dim)
        first = lax.slice_in_dim(x, 0, width, axis=dim)
        before = lax.ppermute(last, axis, up)
        after = lax.ppermute(first, axis, down)
        x = jnp.concatenate([before, x, after], axis=dim)
    return x


def ramp_block(start, width, size):
    row_ids = lax.iota(jnp.int32, size)[:, None]
    col_ids = start + lax.iota(jnp.int32, width)[None, :]
    offset_odd = jnp.abs(row_ids - col_ids) % 2 == 1
    distance = jnp.where(offset_odd, row_ids - col_ids, 1).astype(jnp.float32)
    kernel = jnp.where(
        row_ids == col_ids,
        0.25,
        jnp.where(offset_odd, -1.0 / (math.pi * math.pi * distance * distance), 0.0),
    )
    return kernel.astype(jnp.bfloat16)


def conv_taps(inputs, weights):
    length = inputs.shape[1] - 2
    result = None
    for col_tap in range(3):
        partial_value = None
        for ang_tap in range(3):
            product = jnp.einsum(
                "oc,cau->oau",
                weights[ang_tap, col_tap],
                inputs[:, ang_tap : ang_tap + length],
                preferred_element_type=jnp.float32,
            )
            partial_value = product if partial_value is None else partial_value + product
        if col_tap == 0:
            partial_value = jnp.concatenate(
                [jnp.zeros_like(partial_value[:, :, :1]), partial_value[:, :, :-1]], axis=2
            )
        elif col_tap == 2:
            partial_value = jnp.concatenate(
                [partial_value[:, :, 1:], jnp.zeros_like(partial_value[:, :, :1])], axis=2
            )
        result = partial_value if result is None else result + partial_value
    return result


def conv_layer(inputs, weights, biases):
    return jax.nn.silu(conv_taps(inputs, weights) + biases[:, None, None]).astype(jnp.bfloat16)


def wrap_rims(values):
    return extended(values, (("ang", 2),), 1)


def interpolate(filtered, magnify, detector_shift):
    columns = filtered.shape[2]
    centre = (columns - 1) / 2.0
    places = (
        (lax.iota(jnp.float32, columns)[None, :] - centre) * magnify[:, None]
        + centre
        + detector_shift[:, None]
    )
    floors = jnp.floor(places)
    weight = (places - floors)[:, None, :]
    low_index = jnp.broadcast_to(floors.astype(jnp.int32)[:, None, :], filtered.shape)
    left_vals = jnp.take_along_axis(filtered, low_index, axis=2)
    right_vals = jnp.take_along_axis(filtered, low_index + 1, axis=2)
    return ((1.0 - weight) * left_vals + weight * right_vals).astype(jnp.bfloat16)


def band_starts(slots, offset_row):
    slab_ids = lax.iota(jnp.int32, offset_row.shape[0])
    return jnp.sum(jnp.where(slots[:, None] == slab_ids[None, :], offset_row[None, :], 0), axis=1)


def per_device(
    dual_field,
    forward,
    sinogram,
    first_weight,
    first_bias,
    middle_weight,
    middle_bias,
    last_weight,
    magnify,
    detector_shift,
    row_fraction,
    offsets,
    slab_order,
):
    angles_dev, rows_dev, columns = dual_field.shape
    stacked = jnp.stack([dual_field, forward, sinogram], axis=0).transpose(2, 0, 1, 3)

    def first_rows_layer(row_data):
        return conv_layer(row_data, first_weight, first_bias)

    def middle_rows_layer(row_data):
        return conv_layer(row_data, middle_weight, middle_bias)

    def last_rows_layer(row_data):
        return conv_taps(row_data, last_weight)[0]

    first_act = lax.map(first_rows_layer, wrap_rims(stacked))
    second_act = lax.map(middle_rows_layer, wrap_rims(first_act))
    update = lax.map(last_rows_layer, wrap_rims(second_act))
    new_dual = (dual_field.astype(jnp.float32) + update.transpose(1, 0, 2)).astype(jnp.bfloat16)
    flattened = new_dual.reshape(angles_dev * rows_dev, columns)

    def filter_block(block_id):
        return jnp.dot(
            flattened, ramp_block(block_id * 256, 256, columns), preferred_element_type=jnp.float32
        )

    pieces = lax.map(filter_block, jnp.arange(columns // 256, dtype=jnp.int32))
    filtered = pieces.transpose(1, 0, 2).reshape(angles_dev, rows_dev, columns)
    projected = interpolate(filtered, magnify, detector_shift)
    block_id = lax.axis_index("ang")
    row_id = lax.axis_index("row")
    offset_row = lax.dynamic_slice_in_dim(offsets, block_id, 1, 0)[0]
    depth_pos = lax.iota(jnp.int32, SLAB_Z)
    own_slots = lax.dynamic_slice_in_dim(slab_order, row_id * SLABS_DEV, SLABS_DEV, 0)
    first_rows = (band_starts(own_slots, offset_row)[:, None] + depth_pos[None, :]).reshape(-1)
    keep_weight = (1.0 - row_fraction)[:, None, None]
    take_weight = row_fraction[:, None, None]
    row_piece = lax.all_gather(projected, "row", axis=1, tiled=True)
    piece_rows = lax.iota(jnp.int32, row_piece.shape[1])
    near_rows = (piece_rows[None, :] == first_rows[:, None]).astype(jnp.bfloat16)
    next_rows = (piece_rows[None, :] == first_rows[:, None] + 1).astype(jnp.bfloat16)
    lower_rows = jnp.einsum("kn,anx->akx", near_rows, row_piece, preferred_element_type=jnp.float32)
    upper_rows = jnp.einsum("kn,anx->akx", next_rows, row_piece, preferred_element_type=jnp.float32)
    summed = jnp.sum(keep_weight * lower_rows + take_weight * upper_rows, axis=0)
    combined = lax.psum_scatter(summed, "ang", scatter_dimension=1, tiled=True)
    volume = combined / math.sqrt(angles_dev * lax.axis_size("ang"))
    return (new_dual, volume)


def solution(mesh):
    return jax.shard_map(
        per_device,
        mesh=mesh,
        in_specs=(
            P("ang", "row", None),
            P("ang", "row", None),
            P("ang", "row", None),
            P(),
            P(),
            P(),
            P(),
            P(),
            P("ang"),
            P("ang"),
            P("ang"),
            P(),
            P(),
        ),
        out_specs=(P("ang", "row", None), P("row", "ang")),
        check_vma=False,
    )
```

profile of v0, /device:TPU:1, one launch (start us, length us, event | category | flops | bytes accessed | tf_op | source)
XLA Modules:
  0.0 535.5 jit_solution(8917978119688108449)
XLA Ops:
  8.2 2.7 collective-permute-start
  13.8 1.4 broadcast_compare_fusion.1
  16.5 10.5 %while.42 = (s32[]{:T(128)}, bf16[2,32,4,2048]{3,1,2,0:T(8,128)(2,1)S(1)}, bf16[2,3,6,2048]{3,1,2,0:T(4,128)(2,1)S(1)}, bf16[3,3,32,3]{2,3,1,0:T(4,128)(2,1)}, f32[32]{0:T(128)}, /*index=5*/s32[]{:T(128)}) while((s32[]{:T(128)}, bf16[2,32,4,2048]{3,1,2,0:T(8,128)(2,1)S(1)}, bf16[2,3,6,2048]{3,1,2,0:T(4,128)(2,1)S(1)}, ...), condition=%wide.region_1.2_spmd, body=%wide.region_0.1_spmd.sunk | while | flops 17825792 | bytes 20301716 | solution.py:119
  28.2 4.3 collective-permute-start.3
  34.0 1.4 pad_maximum_fusion.1
  35.4 7.4 %while.43 = (s32[]{:T(128)}, bf16[2,32,4,2048]{3,2,1,0:T(4,128)(2,1)S(1)}, bf16[2,32,6,2048]{3,1,2,0:T(8,128)(2,1)S(1)}, bf16[3,3,32,32]{3,2,1,0:T(8,128)(2,1)S(1)}, f32[32]{0:T(128)S(1)}, /*index=5*/s32[]{:T(128)}) while((s32[]{:T(128)}, bf16[2,32,4,2048]{3,2,1,0:T(4,128)(2,1)S(1)}, bf16[2,32,6,2048]{3,1,2,0:T(8,128)(2,1)S(1)}, ...), condition=%wide.region_3.4_spmd, body=%wide.region_2.3_spmd.sunk | while | flops 154664960 | bytes 26811980 | solution.py:120
  43.7 8.1 %collective-permute-start.5 = (bf16[2,32,1,2048]{3,2,1,0:T(2,128)(2,1)S(1)}, bf16[2,32,1,2048]{3,2,1,0:T(2,128)(2,1)}, u32[]{:S(2)}, u32[]{:S(2)}) collective-permute-start(bf16[2,32,1,2048]{3,2,1,0:T(2,128)(2,1)S(1)} %get-tuple-element.217), channel_id=1, source_target_pairs={{16,0},{32,16},{48,32},{64,48},{80,64},{96,80},{112,96},{128,112},... | collective-permute-start | bytes 786440 | tf_op jit(solution)/shard_map/ppermute | solution.py:20
  53.9 2.9 pad_maximum_fusion
  56.8 12.3 %while.44 = (s32[]{:T(128)}, f32[2,4,2048]{2,0,1:T(2,128)}, bf16[2,32,6,2048]{3,2,1,0:T(8,128)(2,1)S(1)}, bf16[3,3,1,32]{3,2,1,0:T(2,128)(2,1)S(1)}, s32[]{:T(128)}, /*index=5*/s32[]{:T(128)}) while((s32[]{:T(128)}, f32[2,4,2048]{2,0,1:T(2,128)}, bf16[2,32,6,2048]{3,2,1,0:T(8,128)(2,1)S(1)}, bf16[3,3,1,32]{3,2,1,0:T(2,128)(2,1)S(1)}, ...), condition=%wide.region_5.6_spmd, body=%wide.region_4.5_spmd.sunk | while | flops 4784130 | bytes 10392077 | solution.py:121
  61.4 1.6 dynamic_update_slice.27
  67.5 1.6 dynamic_update_slice.27
  70.6 24.4 %while.45 = (s32[]{:T(128)}, f32[8,8,256]{2,1,0:T(8,128)S(1)}, s32[8]{0:T(128)S(1)}, bf16[8,2048]{1,0:T(8,128)(2,1)S(1)}, s32[]{:T(128)}, /*index=5*/s32[1]{0:T(128)}) while((s32[]{:T(128)}, f32[8,8,256]{2,1,0:T(8,128)S(1)}, s32[8]{0:T(128)S(1)}, bf16[8,2048]{1,0:T(8,128)(2,1)S(1)}, s32[]{:T(128)}, /*index=5*/s32[1]{0:T(128)}) %tuple.107), condition=%wide.region_7.8_spmd, body=%wide.region_6.7_spmd.sunk | while | flops 20447492 | bytes 43109 | solution.py:130
  71.8 1.9 fusion.327
  74.8 1.9 fusion.327
  77.9 1.9 fusion.327
  80.9 1.9 fusion.327
  84.0 1.9 fusion.327
  87.0 1.9 fusion.327
  90.0 1.9 fusion.327
  93.1 1.9 fusion.327
  95.1 160.1 %gather_fusion = f32[16384]{0:T(1024)S(1)} fusion(f32[4,2,2048]{2,1,0:T(2,128)S(1)} %reshape.212, s32[16384]{0:T(1024)S(1)} %bitcast.415), kind=kCustom, calls=%fused_computation.clone | custom fusion | bytes 327680 | tf_op jit(solution)/shard_map/jit(take_along_axis)/gather | solution.py:82
  255.2 160.1 %gather_fusion.1 = f32[16384]{0:T(1024)S(1)} fusion(f32[4,2,2048]{2,1,0:T(2,128)S(1)} %reshape.212, s32[16384]{0:T(1024)S(1)} %bitcast.414), kind=kCustom, calls=%fused_computation.1.clone | custom fusion | bytes 327680 | tf_op jit(solution)/shard_map/jit(take_along_axis)/gather | solution.py:83
  415.6 31.2 %all_gather.3 = bf16[4,32,2048]{2,0,1:T(4,128)(2,1)S(1)} all-gather(bf16[4,2,2048]{2,0,1:T(4,128)(2,1)S(1)} %copy.56), channel_id=1, replica_groups=mesh['ang'=16,'row'=16] {'row'}, dimensions={1}, use_global_device_ids=true | all-gather | bytes 557056 | tf_op jit(solution)/shard_map/all_gather | solution.py:141
  448.4 79.0 %reduce-scatter.2.cloned.1.call-done = f32[16,128]{1,0:T(8,128)} async-done(((f32[16,2048]{1,0:T(8,128)}), f32[16,128]{1,0:T(8,128)}) %reduce-scatter.2.cloned.1.call-update) | async-done | bytes 8208 | tf_op jit(solution)/shard_map/reduce_scatter | solution.py:148
  (183 shorter events, 46.4 us)
Async XLA Ops:
  7.2 8.0 %copy-start = (s32[16,64]{1,0:T(8,128)S(1)}, s32[16,64]{1,0:T(8,128)}, u32[]{:S(2)}) copy-start(s32[16,64]{1,0:T(8,128)} %param.34) | copy-start | bytes 12292
  7.2 520.2 %reduce-scatter.2.cloned.1.call-start = ((), (), s32[]{:S(2)}) async-start(), calls=%async_computation.1 | async-start | bytes 139264 | tf_op jit(solution)/shard_map/reduce_scatter | solution.py:148
  8.2 7.9 %collective-permute-start = (bf16[2,3,1,2048]{3,0,2,1:T(2,128)(2,1)S(1)}, bf16[2,3,1,2048]{3,0,2,1:T(2,128)(2,1)S(1)}, u32[]{:S(2)}, u32[]{:S(2)}) collective-permute-start(bf16[2,3,1,2048]{3,0,2,1:T(2,128)(2,1)S(1)} %get-tuple-element.220), channel_id=1, source_target_pairs={{0,16},{16,32},{32,48},{48,64},{64,80},{80,96},{96,112},{112,128},... | collective-permute-start | bytes 73736 | tf_op jit(solution)/shard_map/ppermute | solution.py:19
  10.9 5.2 collective-permute-start.1
  21.8 2.1 copy-start.4
  27.0 6.6 %copy-start.1 = (bf16[2,32,4,2048]{3,1,2,0:T(8,128)(2,1)}, bf16[2,32,4,2048]{3,1,2,0:T(8,128)(2,1)S(1)}, u32[]{:S(2)}) copy-start(bf16[2,32,4,2048]{3,1,2,0:T(8,128)(2,1)S(1)} %get-tuple-element.133) | copy-start | bytes 3145732
  27.0 8.4 %copy-start.2 = (bf16[3,3,32,32]{3,2,1,0:T(8,128)(2,1)S(1)}, bf16[3,3,32,32]{3,2,1,0:T(8,128)(2,1)}, u32[]{:S(2)}) copy-start(bf16[3,3,32,32]{3,2,1,0:T(8,128)(2,1)} %param.28) | copy-start | bytes 55300
  27.0 8.4 %copy-start.19 = (f32[32]{0:T(128)S(1)}, f32[32]{0:T(128)}, u32[]{:S(2)}) copy-start(f32[32]{0:T(128)} %param.29) | copy-start | bytes 388
  27.1 6.5 %collective-permute-start.2 = (bf16[2,32,1,2048]{3,1,2,0:T(8,128)(2,1)S(1)}, bf16[2,32,1,2048]{3,1,2,0:T(8,128)(2,1)S(1)}, u32[]{:S(2)}, u32[]{:S(2)}) collective-permute-start(bf16[2,32,1,2048]{3,1,2,0:T(8,128)(2,1)S(1)} %get-tuple-element.218), channel_id=1, source_target_pairs={{0,16},{16,32},{32,48},{48,64},{64,80},{80,96},{96,112},{112,128},... | collective-permute-start | bytes 786440 | tf_op jit(solution)/shard_map/ppermute | solution.py:19
  28.2 5.8 %collective-permute-start.3 = (bf16[2,32,1,2048]{3,1,2,0:T(8,128)(2,1)S(1)}, bf16[2,32,1,2048]{3,1,2,0:T(8,128)(2,1)S(1)}, u32[]{:S(2)}, u32[]{:S(2)}) collective-permute-start(bf16[2,32,1,2048]{3,1,2,0:T(8,128)(2,1)S(1)} %get-tuple-element.219), channel_id=1, source_target_pairs={{16,0},{32,16},{48,32},{64,48},{80,64},{96,80},{112,96},{128,112},... | collective-permute-start | bytes 786440 | tf_op jit(solution)/shard_map/ppermute | solution.py:20
  32.7 19.1 %copy-start.13 = (s32[16]{0:T(128)}, s32[16]{0:T(128)S(1)}, u32[]{:S(2)}) copy-start(s32[16]{0:T(128)S(1)} %add.297) | copy-start | bytes 196
  42.8 9.6 %copy-start.12 = (bf16[3,3,1,32]{3,1,2,0:T(4,128)(2,1)S(1)}, bf16[3,3,1,32]{3,1,2,0:T(4,128)(2,1)}, u32[]{:S(2)}) copy-start(bf16[3,3,1,32]{3,1,2,0:T(4,128)(2,1)} %param.30) | copy-start | bytes 1732
  42.8 10.2 %copy-start.15 = (f32[4]{0:T(128)S(1)}, f32[4]{0:T(128)}, u32[]{:S(2)}) copy-start(f32[4]{0:T(128)} %param.33) | copy-start | bytes 52
  43.6 9.5 %collective-permute-start.4 = (bf16[2,32,1,2048]{3,2,1,0:T(2,128)(2,1)S(1)}, bf16[2,32,1,2048]{3,2,1,0:T(2,128)(2,1)S(1)}, u32[]{:S(2)}, u32[]{:S(2)}) collective-permute-start(bf16[2,32,1,2048]{3,2,1,0:T(2,128)(2,1)S(1)} %get-tuple-element.216), channel_id=1, source_target_pairs={{0,16},{16,32},{32,48},{48,64},{64,80},{80,96},{96,112},{112,128},... | collective-permute-start | bytes 786440 | tf_op jit(solution)/shard_map/ppermute | solution.py:19
  43.7 10.2 %collective-permute-start.5 = (bf16[2,32,1,2048]{3,2,1,0:T(2,128)(2,1)S(1)}, bf16[2,32,1,2048]{3,2,1,0:T(2,128)(2,1)}, u32[]{:S(2)}, u32[]{:S(2)}) collective-permute-start(bf16[2,32,1,2048]{3,2,1,0:T(2,128)(2,1)S(1)} %get-tuple-element.217), channel_id=1, source_target_pairs={{16,0},{32,16},{48,32},{64,48},{80,64},{96,80},{112,96},{128,112},... | collective-permute-start | bytes 786440 | tf_op jit(solution)/shard_map/ppermute | solution.py:20
  53.0 3.8 copy-start.11
  56.8 12.3 %copy-start.8 = (bf16[4,2,2048]{2,1,0:T(2,128)(2,1)S(1)}, bf16[4,2,2048]{2,1,0:T(2,128)(2,1)}, u32[]{:S(2)}) copy-start(bf16[4,2,2048]{2,1,0:T(2,128)(2,1)} %param.23) | copy-start | bytes 98308
  56.8 13.2 %copy-start.10 = (f32[8,8,256]{2,1,0:T(8,128)S(1)}, f32[8,8,256]{2,1,0:T(8,128)}, u32[]{:S(2)}) copy-start(f32[8,8,256]{2,1,0:T(8,128)} %custom-call.9) | copy-start | bytes 196612
  255.2 160.2 %copy-start.5 = (f32[4,2048]{1,0:T(4,128)S(1)}, f32[4,2048]{1,0:T(4,128)}, u32[]{:S(2)}) copy-start(f32[4,2048]{1,0:T(4,128)} %get-tuple-element.222) | copy-start | bytes 98308
  255.2 160.2 %copy-start.6 = (f32[4,2048]{1,0:T(4,128)S(1)}, f32[4,2048]{1,0:T(4,128)}, u32[]{:S(2)}) copy-start(f32[4,2048]{1,0:T(4,128)} %get-tuple-element.223) | copy-start | bytes 98308
  255.2 160.2 %copy-start.9 = (pred[4,2048]{1,0:T(4,128)(4,1)S(1)}, pred[4,2048]{1,0:T(4,128)(4,1)}, u32[]{:S(2)}) copy-start(pred[4,2048]{1,0:T(4,128)(4,1)} %get-tuple-element.229) | copy-start | bytes 24580
  255.2 191.6 %copy-start.16 = (f32[4]{0:T(128)S(1)}, f32[4]{0:T(128)}, u32[]{:S(2)}) copy-start(f32[4]{0:T(128)} %param.33) | copy-start | bytes 52
  255.2 191.6 %copy-start.17 = (s32[16]{0:T(128)S(1)}, s32[16]{0:T(128)}, u32[]{:S(2)}) copy-start(s32[16]{0:T(128)} %broadcast_add_fusion.3) | copy-start | bytes 196
  415.3 32.0 %copy-start.14 = (s32[16]{0:T(128)S(1)}, s32[16]{0:T(128)}, u32[]{:S(2)}) copy-start(s32[16]{0:T(128)} %copy-done.13) | copy-start | bytes 196
  (5 other events, 5.0 us)
Sparse Core Ops, SparseCore 0:
  448.5 78.8 reduce-scatter.1
where the time goes:
time: 537 us; the launch traced here: 536 us
  local copies, waits for them, and re-layouts  336 us (63%)
  waiting for transfers between devices  79.4 us (15%)
  matrix products  38.7 us (7%)
  blocking collectives  31.2 us (6%)
  starting transfers between devices  17.1 us (3%)
  between operations  14.5 us (3%)
  other arithmetic  13.4 us (2%)
    gather x2, local copies, waits for them, and re-layouts, interpolate(): left_vals = jnp.take_along_axis(filtered, low_index, axis=2)  160 us
    gather x2, local copies, waits for them, and re-layouts, interpolate(): right_vals = jnp.take_along_axis(filtered, low_index + 1, axis=2)  160 us
    reduce_scatter x1, waiting for transfers between devices, per_device(): combined = lax.psum_scatter(summed, 'ang', scatter_dimension=1, tiled=True)  79 us
    all_gather x1, blocking collectives, per_device(): row_piece = lax.all_gather(projected, 'row', axis=1, tiled=True)  31.2 us
    dot_general x54, matrix products, conv_taps(): jnp.einsum('oc,cau->oau', weights[ang_tap, col_tap], inputs[:, ang_tap:an...  22.2 us
    dot_general x8, matrix products, filter_block(): jnp.dot(flattened, ramp_block(block_id * 256, 256, columns), preferred_el...  15 us
    ppermute x3, starting transfers between devices, extended(): after = lax.ppermute(first, axis, down)  13.2 us
  transfers between devices with their start and end apart: 7, of which 2 were waited for; matrix products, arithmetic and copies ran while one was open for 1% of the time, Pallas kernels for 0%

commit v1 on v0

v1 whole, which is shorter than its diff:
```python
import math

import jax
import jax.numpy as jnp
import numpy as np
from jax import lax
from jax.experimental import pallas as pl
from jax.experimental.pallas import tpu as pltpu
from jax.sharding import PartitionSpec as P

U = 2048
CH = 32
ANG_DEV = 4
ROWS_DEV = 2
HALO = 3
FIELDS = 3
SLAB_Z = 4
SLABS_DEV = 4
BLOCKS = 16
ROW_DEVS = 16
LANES = 128
TILES = U // LANES
BLK = 256
NBLK = U // BLK
SPAN = ANG_DEV + 2 * HALO
ROWS1 = ROWS_DEV * (SPAN - 2) * CH
HALF1 = (SPAN - 2) * CH
HALF2 = (SPAN - 4) * CH
OUT8 = ANG_DEV * ROWS_DEV
CENTRE = (U - 1) / 2.0
MIB = 1024 * 1024
MAG_LOW, MAG_HIGH, SHIFT_MAX = 0.85, 0.95, 8.0


def ramp_tiles():
    row_ids = np.arange(BLK, dtype=np.int32)[None, :, None]
    col_ids = np.arange(BLK, dtype=np.int32)[None, None, :]
    gaps = np.arange(-(NBLK - 1), NBLK, dtype=np.int32)[:, None, None] * BLK
    diff = row_ids - (col_ids + gaps)
    odd = np.abs(diff) % 2 == 1
    distance = np.where(odd, diff, 1).astype(np.float32)
    falloff = np.float32(-1.0) / (np.float32(math.pi * math.pi) * distance * distance)
    tiles = np.where(diff == 0, np.float32(0.25), np.where(odd, falloff, np.float32(0.0)))
    return jnp.asarray(tiles.astype(np.float32)).astype(jnp.bfloat16)


def shifted(value, step):
    lane = lax.broadcasted_iota(jnp.int32, value.shape, 1)
    if step < 0:
        return jnp.where(lane == 0, 0.0, pltpu.roll(value, 1, 1))
    return jnp.where(lane == U - 1, 0.0, pltpu.roll(value, U - 1, 1))


def silu(value):
    half = 0.5 * value
    return half + half * jnp.tanh(half)


def source_tiles(tile):
    ends = []
    for column in (tile * LANES, tile * LANES + LANES - 1):
        for mag in (MAG_LOW, MAG_HIGH):
            for shift in (-SHIFT_MAX, SHIFT_MAX):
                ends.append((column - CENTRE) * mag + CENTRE + shift)
    low = int(math.floor(min(ends) - 0.5))
    high = int(math.floor(max(ends) + 0.5)) + 1
    return max(low, 0) // LANES, min(high, U - 1) // LANES


def pack_kernel(dual_hbm, forw_hbm, sino_hbm, out_ref, sems):
    loads = [
        pltpu.make_async_copy(field, out_ref.at[pl.ds(at * ANG_DEV, ANG_DEV)], sems.at[at])
        for at, field in enumerate((dual_hbm, forw_hbm, sino_hbm))
    ]
    for load in loads:
        load.start()
    for load in loads:
        load.wait()


def layout_kernel(
    first_ref, middle_ref, last_ref, bias1_ref, bias2_ref, order_ref, offs_ref,
    w1_ref, w2_ref, w3_ref, col1_ref, col2_ref, pick_ref,
    gather1, base2, base3,
):
    f32, bf16 = jnp.float32, jnp.bfloat16
    gather1[...] = jnp.zeros(gather1.shape, f32)
    for part in range(9):
        gather1[3 * part:3 * part + 3, 0:CH] = first_ref[part].astype(f32)
    key = lax.broadcasted_iota(jnp.int32, (32, 256), 0)
    lane = lax.broadcasted_iota(jnp.int32, (32, 256), 1)
    wanted = (key // 3 % 3) * 64 + (key % 3) * (2 * SPAN) + (key // 9) * 2
    spread = jnp.where((lane == wanted) & (key < 27), 1.0, 0.0)
    base1 = lax.dot_general(
        gather1[...].astype(bf16), spread.astype(bf16), (((0,), (0,)), ((), ())), preferred_element_type=f32
    )[0:CH]
    for row in range(ROWS_DEV):
        for ang in range(SPAN - 2):
            shift = 2 * ang + row
            rolled = pltpu.roll(base1, shift, 1) if shift else base1
            start = (row * (SPAN - 2) + ang) * CH
            w1_ref[start:start + CH, :] = rolled.astype(bf16)
    base2[...] = jnp.zeros(base2.shape, f32)
    for ang_tap in range(3):
        for tap in range(3):
            block = middle_ref[3 * ang_tap + tap].astype(f32)
            base2[tap * CH:(tap + 1) * CH, ang_tap * CH:(ang_tap + 1) * CH] = block
    for tap in range(3):
        wide = base2[tap * CH:(tap + 1) * CH, :]
        for ang in range(SPAN - 4):
            rolled = pltpu.roll(wide, CH * ang, 1) if ang else wide
            start = tap * HALF2 + ang * CH
            w2_ref[start:start + CH, :] = rolled.astype(bf16)
    base3[...] = jnp.zeros(base3.shape, f32)
    for ang_tap in range(3):
        base3[0:3, ang_tap * CH:(ang_tap + 1) * CH] = last_ref[ang_tap].astype(f32)
    wide = base3[...]
    for ang in range(ANG_DEV):
        for row in range(ROWS_DEV):
            shift = CH * ang + HALF2 * row
            rolled = pltpu.roll(wide, shift, 1) if shift else wide
            for tap in range(3):
                at = tap * OUT8 + ang * ROWS_DEV + row
                w3_ref[at:at + 1, :] = rolled[tap:tap + 1, :]
    square = (CH, CH)
    eye = lax.broadcasted_iota(jnp.int32, square, 0) == lax.broadcasted_iota(jnp.int32, square, 1)
    for bias_ref, col_ref in ((bias1_ref, col1_ref), (bias2_ref, col2_ref)):
        column = jnp.sum(jnp.where(eye, jnp.broadcast_to(bias_ref[...], square), 0.0), axis=1, keepdims=True)
        col_ref[...] = jnp.broadcast_to(column, (CH, LANES))
    slabs = SLABS_DEV * ROW_DEVS
    chosen = jnp.broadcast_to(order_ref[...], (slabs, slabs)) == lax.broadcasted_iota(jnp.int32, (slabs, slabs), 0)
    chosen = jnp.where(chosen, 1.0, 0.0).astype(bf16)
    starts = jnp.dot(offs_ref[...].astype(f32).astype(bf16), chosen, preferred_element_type=f32)
    width = 3 * 4 * BLOCKS
    block_of = (lax.broadcasted_iota(jnp.int32, (BLOCKS, width), 1) % (4 * BLOCKS)) // 4
    widen = jnp.where(block_of == lax.broadcasted_iota(jnp.int32, (BLOCKS, width), 0), 1.0, 0.0).astype(bf16)
    starts = lax.dot_general(
        starts.astype(bf16), widen, (((0,), (0,)), ((), ())), preferred_element_type=f32
    )
    rows = slabs * SLAB_Z
    slot_of = lax.broadcasted_iota(jnp.int32, (rows, slabs), 0) // SLAB_Z
    tall = jnp.where(slot_of == lax.broadcasted_iota(jnp.int32, (rows, slabs), 1), 1.0, 0.0).astype(bf16)
    starts = jnp.dot(tall, starts.astype(bf16), preferred_element_type=f32)
    depth = lax.broadcasted_iota(jnp.int32, (rows, width), 0) % SLAB_Z
    kind = lax.broadcasted_iota(jnp.int32, (rows, width), 1) % 4
    offset = depth + kind // 2 - kind % 2 - ROWS_DEV * lax.axis_index("row")
    pick_ref[...] = jnp.where(starts + offset.astype(f32) == 0.0, 1.0, 0.0).astype(bf16)


def field_kernel(
    mag_hbm, move_hbm, frac_hbm, ramp_hbm, own_ref, even_ref, odd_ref,
    w1_ref, w2_ref, w3_ref, col1_ref, col2_ref,
    dual_hbm, send_ref,
    x32, xcat, act1, taps2, act2, ramp_ref, dual_ref, mag_ref, move_ref, frac_ref, sems,
):
    f32, bf16 = jnp.float32, jnp.bfloat16
    loads = [
        pltpu.make_async_copy(mag_hbm, mag_ref, sems.at[0]),
        pltpu.make_async_copy(move_hbm, move_ref, sems.at[1]),
        pltpu.make_async_copy(frac_hbm, frac_ref, sems.at[2]),
        pltpu.make_async_copy(ramp_hbm, ramp_ref, sems.at[3]),
    ]
    for load in loads:
        load.start()
    x32[3 * 2 * SPAN:64, :] = jnp.zeros((64 - 3 * 2 * SPAN, U), f32)

    def lay(left_ref, right_ref):
        for field in range(FIELDS):
            base = field * 2 * SPAN
            for ang in range(HALO):
                x32[base + 2 * ang:base + 2 * ang + 2, :] = left_ref[field * ANG_DEV + 1 + ang].astype(f32)
                at = base + 2 * (HALO + ANG_DEV + ang)
                x32[at:at + 2, :] = right_ref[field * ANG_DEV + ang].astype(f32)

    for field in range(FIELDS):
        for ang in range(ANG_DEV):
            at = field * 2 * SPAN + 2 * (HALO + ang)
            x32[at:at + 2, :] = own_ref[field * ANG_DEV + ang].astype(f32)
    parity = lax.axis_index("ang") % 2

    @pl.when(parity == 0)
    def _():
        lay(odd_ref, even_ref)

    @pl.when(parity == 1)
    def _():
        lay(even_ref, odd_ref)

    stacked = x32[...]
    xcat[0:64, :] = shifted(stacked, -1).astype(bf16)
    xcat[64:128, :] = stacked.astype(bf16)
    xcat[128:192, :] = shifted(stacked, 1).astype(bf16)
    xcat[192:256, :] = jnp.zeros((64, U), bf16)

    bias1 = col1_ref[:, 0:1]

    def first_layer(step, carry):
        cols = pl.ds(pl.multiple_of(step * BLK, BLK), BLK)
        block = jnp.dot(w1_ref[...], xcat[:, cols], preferred_element_type=f32)
        for part in range(ROWS1 // CH):
            rows = slice(part * CH, (part + 1) * CH)
            act1[rows, cols] = silu(block[rows] + bias1).astype(bf16)
        return carry

    lax.fori_loop(0, NBLK, first_layer, 0)

    def second_dots(step, carry):
        cols = pl.ds(pl.multiple_of(step * BLK, BLK), BLK)
        for row in range(ROWS_DEV):
            taps2[row, :, cols] = jnp.dot(
                w2_ref[...], act1[row * HALF1:(row + 1) * HALF1, cols], preferred_element_type=f32
            )
        return carry

    lax.fori_loop(0, NBLK, second_dots, 0)

    bias2 = col2_ref[:, 0:1]

    def second_sum(step, carry):
        start = pl.multiple_of(step * CH, CH)
        for row in range(ROWS_DEV):
            before = shifted(taps2[row, pl.ds(start, CH), :], -1)
            here = taps2[row, pl.ds(HALF2 + start, CH), :]
            after = shifted(taps2[row, pl.ds(2 * HALF2 + start, CH), :], 1)
            total = before + here + after + bias2
            act2[pl.ds(row * HALF2 + start, CH), :] = silu(total).astype(bf16)
        return carry

    lax.fori_loop(0, HALF2 // CH, second_sum, 0)

    taps3 = jnp.dot(w3_ref[...].astype(bf16), act2[...], preferred_element_type=f32)
    update = shifted(taps3[0:8], -1) + taps3[8:16] + shifted(taps3[16:24], 1)
    own_dual = x32[2 * HALO:2 * HALO + OUT8, :]
    new_dual = (own_dual + update).astype(bf16)
    for ang in range(ANG_DEV):
        dual_ref[ang] = new_dual[2 * ang:2 * ang + 2, :]
    store = pltpu.make_async_copy(dual_ref, dual_hbm, sems.at[4])
    store.start()
    for load in loads:
        load.wait()
    dual32 = new_dual.astype(f32)
    blocks = jnp.concatenate([dual32[:, b * BLK:(b + 1) * BLK] for b in range(NBLK)], axis=0).astype(bf16)
    filtered = [None] * NBLK
    for gap in range(-(NBLK - 1), NBLK):
        part = jnp.dot(blocks, ramp_ref[gap + NBLK - 1], preferred_element_type=f32)
        for source in range(NBLK):
            target = source + gap
            if 0 <= target < NBLK:
                piece = part[source * OUT8:(source + 1) * OUT8]
                filtered[target] = piece if filtered[target] is None else filtered[target] + piece
    lanes = [filtered[t // 2][:, (t % 2) * LANES:(t % 2 + 1) * LANES] for t in range(TILES)]
    row_id = lax.broadcasted_iota(jnp.int32, (OUT8, LANES), 0)
    lane_id = lax.broadcasted_iota(jnp.int32, (OUT8, LANES), 1)
    ang_id = row_id // ROWS_DEV

    def per_angle(ref):
        value = jnp.full((OUT8, LANES), ref[0], f32)
        for ang in range(1, ANG_DEV):
            value = jnp.where(ang_id == ang, ref[ang], value)
        return value

    mag, move, frac = per_angle(mag_ref), per_angle(move_ref), per_angle(frac_ref)
    keep = 1.0 - frac
    for tile in range(TILES):
        column = (lane_id + tile * LANES).astype(f32)
        place = (column - CENTRE) * mag + CENTRE + move
        floor = jnp.floor(place)
        weight = place - floor
        low = floor.astype(jnp.int32)
        high = low + 1
        first, last = source_tiles(tile)
        left = jnp.zeros((OUT8, LANES), f32)
        right = jnp.zeros((OUT8, LANES), f32)
        for source in range(first, last + 1):
            got = jnp.take_along_axis(lanes[source], low & (LANES - 1), axis=1, mode="promise_in_bounds")
            left = jnp.where(low // LANES == source, got, left)
            got = jnp.take_along_axis(lanes[source], high & (LANES - 1), axis=1, mode="promise_in_bounds")
            right = jnp.where(high // LANES == source, got, right)
        projected = ((1.0 - weight) * left + weight * right).astype(bf16).astype(f32)
        lower = keep * projected
        upper = frac * projected
        lower = lower + pltpu.roll(lower, 4, 0)
        lower = lower + pltpu.roll(lower, 2, 0)
        upper = upper + pltpu.roll(upper, 4, 0)
        upper = upper + pltpu.roll(upper, 2, 0)
        packed = jnp.where(row_id < ROWS_DEV, lower, upper)
        send_ref[tile] = packed[0:4]
    store.wait()


def place_kernel(pick_ref, got_ref, out_ref):
    f32, bf16 = jnp.float32, jnp.bfloat16
    rows = got_ref[...]
    high = rows.astype(bf16)
    rest = rows - high.astype(f32)
    mid = rest.astype(bf16)
    low = (rest - mid.astype(f32)).astype(bf16)
    parts = jnp.concatenate([high, mid, low], axis=0)
    out_ref[...] = jnp.dot(pick_ref[...], parts, preferred_element_type=f32)


def in_hbm(value):
    return pltpu.with_memory_space_constraint(value, pltpu.HBM)


def per_device(
    dual_field, forward, sinogram, first_weight, first_bias, middle_weight, middle_bias, last_weight,
    magnify, detector_shift, row_fraction, offsets, slab_order,
):
    f32, bf16 = jnp.float32, jnp.bfloat16
    vmem = pl.BlockSpec(memory_space=pltpu.VMEM)
    hbm = pl.BlockSpec(memory_space=pltpu.HBM)
    own = pl.pallas_call(
        pack_kernel,
        out_shape=jax.ShapeDtypeStruct((FIELDS * ANG_DEV, ROWS_DEV, U), bf16),
        in_specs=[hbm] * 3,
        out_specs=vmem,
        scratch_shapes=[pltpu.SemaphoreType.DMA((3,))],
        compiler_params=pltpu.CompilerParams(vmem_limit_bytes=2 * MIB),
        name="pack_kernel",
    )(*map(in_hbm, (dual_field, forward, sinogram)))
    count = lax.axis_size("ang")
    even = lax.ppermute(own, "ang", [(i, i ^ 1) for i in range(count)])
    odd = lax.ppermute(own, "ang", [(i, (i + 1 if i % 2 else i - 1) % count) for i in range(count)])
    width = 3 * 4 * BLOCKS
    w1, w2, w3, col1, col2, pick = pl.pallas_call(
        layout_kernel,
        out_shape=(
            jax.ShapeDtypeStruct((ROWS1, 256), bf16),
            jax.ShapeDtypeStruct((3 * HALF2, HALF1), bf16),
            jax.ShapeDtypeStruct((24, 2 * HALF2), f32),
            jax.ShapeDtypeStruct((CH, LANES), f32),
            jax.ShapeDtypeStruct((CH, LANES), f32),
            jax.ShapeDtypeStruct((SLABS_DEV * ROW_DEVS * SLAB_Z, width), bf16),
        ),
        out_specs=(vmem,) * 6,
        scratch_shapes=[
            pltpu.VMEM((32, LANES), f32),
            pltpu.VMEM((3 * CH, HALF1), f32),
            pltpu.VMEM((8, 2 * HALF2), f32),
        ],
        compiler_params=pltpu.CompilerParams(vmem_limit_bytes=8 * MIB),
        name="layout_kernel",
    )(*map(in_hbm, (
        first_weight.transpose(0, 1, 3, 2).reshape(9, FIELDS, CH), middle_weight.reshape(9, CH, CH),
        last_weight.transpose(0, 2, 1, 3).reshape(3, 3, CH), first_bias[None], middle_bias[None],
        slab_order[None], offsets,
    )))
    new_dual, send = pl.pallas_call(
        field_kernel,
        out_shape=(
            jax.ShapeDtypeStruct((ANG_DEV, ROWS_DEV, U), bf16),
            jax.ShapeDtypeStruct((BLOCKS, 4, LANES), f32),
        ),
        in_specs=[hbm] * 4 + [vmem] * 8,
        out_specs=(hbm, vmem),
        scratch_shapes=[
            pltpu.VMEM((64, U), f32),
            pltpu.VMEM((256, U), bf16),
            pltpu.VMEM((ROWS1, U), bf16),
            pltpu.VMEM((ROWS_DEV, 3 * HALF2, U), f32),
            pltpu.VMEM((2 * HALF2, U), bf16),
            pltpu.VMEM((2 * NBLK - 1, BLK, BLK), bf16),
            pltpu.VMEM((ANG_DEV, ROWS_DEV, U), bf16),
            pltpu.SMEM((ANG_DEV,), f32),
            pltpu.SMEM((ANG_DEV,), f32),
            pltpu.SMEM((ANG_DEV,), f32),
            pltpu.SemaphoreType.DMA((5,)),
        ],
        compiler_params=pltpu.CompilerParams(vmem_limit_bytes=32 * MIB),
        name="field_kernel",
    )(*map(in_hbm, (magnify, detector_shift, row_fraction, ramp_tiles())), own, even, odd, w1, w2, w3, col1, col2)
    got = lax.all_to_all(send, "ang", 0, 0, tiled=True)
    placed = pl.pallas_call(
        place_kernel,
        out_shape=jax.ShapeDtypeStruct((SLABS_DEV * ROW_DEVS * SLAB_Z, LANES), f32),
        in_specs=[vmem, vmem],
        out_specs=vmem,
        compiler_params=pltpu.CompilerParams(vmem_limit_bytes=4 * MIB),
        name="place_kernel",
    )(pick, got.reshape(4 * BLOCKS, LANES))
    shares = lax.all_to_all(placed.reshape(ROW_DEVS, SLABS_DEV * SLAB_Z, LANES), "row", 0, 0, tiled=True)
    return new_dual, jnp.sum(shares, axis=0) * 0.125


def solution(mesh):
    field = P("ang", "row", None)
    return jax.shard_map(
        per_device,
        mesh=mesh,
        in_specs=(field, field, field) + (P(),) * 5 + (P("ang"),) * 3 + (P(), P()),
        out_specs=(field, P("row", "ang")),
        check_vma=False,
    )
```

time: 537 us -> 50.3 us (0.09)
  local copies, waits for them, and re-layouts: 336 us -> 0 us
  waiting for transfers between devices: 79.4 us -> 0.01 us
  matrix products: 38.7 us -> 0 us
  between operations: 14.5 us -> 0.68 us
  other arithmetic: 13.4 us -> 0.62 us
  Pallas kernels: 0 us -> 11.1 us
  starting transfers between devices: 17.1 us -> 6.42 us
    gather x4 -> x0, local copies, waits for them, and re-layouts: 320 us -> none  [the longest x2 160 us: interpolate(): left_vals = jnp.take_along_axis(filtered, low_index, axis=2)]
    reduce_scatter x1 -> x0, waiting for transfers between devices: 79 us -> none  [per_device(): combined = lax.psum_scatter(summed, 'ang', scatter_dimension=1, tiled=True)]
    dot_general x64 -> x0, matrix products: 38.7 us -> none  [the longest x54 22.2 us: conv_taps(): jnp.einsum('oc,cau->oau', weights[ang_tap, col_tap], inputs[:, ang_tap:an...]
    all_gather x1 -> x0, blocking collectives: 31.2 us -> none  [per_device(): row_piece = lax.all_gather(projected, 'row', axis=1, tiled=True)]
    all_to_all x0 -> x2, blocking collectives: none -> 31.2 us  [the longest x1 16.7 us: per_device(): lax.all_to_all(placed.reshape(ROW_DEVS, SLABS_DEV * SLAB_Z, LANES), 'row'...]
    pallas_call x0 -> x4, Pallas kernels: none -> 11.1 us  [the longest x1 8.66 us: per_device(): pl.pallas_call(field_kernel, out_shape=(jax.ShapeDtypeStruct((ANG_DEV, RO...]
    ppermute x6 -> x2, starting transfers between devices: 17.1 us -> 6.42 us  [the longest x1 3.73 us: per_device(): even = lax.ppermute(own, 'ang', [(i, i ^ 1) for i in range(count)])]
    dynamic_slice x9 -> x0, local copies, waits for them, and re-layouts: 5.39 us -> none  [the longest x8 4.65 us: per_device(): pieces = lax.map(filter_block, jnp.arange(columns // 256, dtype=jnp.int32))]
  transfers between devices with their start and end apart: 7 -> 2, of which waited for: 2 -> 0; matrix products, arithmetic and copies ran while one was open for 1% -> 0% of each run, Pallas kernels for 0% -> 3%
where the time goes in v1:
time: 50.3 us; the launch traced here: 50 us
  blocking collectives  31.2 us (62%)
  Pallas kernels  11.1 us (22%)
  starting transfers between devices  6.42 us (13%)
  between operations  0.68 us (1%)
  other arithmetic  0.62 us (1%)
    all_to_all x1, blocking collectives, per_device(): lax.all_to_all(placed.reshape(ROW_DEVS, SLABS_DEV * SLAB_Z, LANES), 'row'...  16.7 us
    all_to_all x1, blocking collectives, per_device(): got = lax.all_to_all(send, 'ang', 0, 0, tiled=True)  14.5 us
    pallas_call x1, Pallas kernels, per_device(): pl.pallas_call(field_kernel, out_shape=(jax.ShapeDtypeStruct((ANG_DEV, RO...  8.66 us
    ppermute x1, starting transfers between devices, per_device(): even = lax.ppermute(own, 'ang', [(i, i ^ 1) for i in range(count)])  3.73 us
    ppermute x1, starting transfers between devices, per_device(): lax.ppermute(own, 'ang', [(i, (i + 1 if i % 2 else i - 1) % count) for i...  2.69 us
    pallas_call x1, Pallas kernels, per_device(): pl.pallas_call(layout_kernel, out_shape=(jax.ShapeDtypeStruct((ROWS1, 256...  1.46 us
  transfers between devices with their start and end apart: 2, of which 0 were waited for; matrix products, arithmetic and copies ran while one was open for 0% of the time, Pallas kernels for 3%

profile of v1, /device:TPU:1, one launch (start us, length us, event | category | flops | bytes accessed | tf_op | source)
XLA Modules:
  0.0 50.0 jit_solution(1002851149393864924)
XLA Ops:
  0.6 0.8 %pack_kernel.1.own_ref = bf16[12,2,2048]{2,1,0:T(2,128)(2,1)S(1)} custom-call(bf16[4,2,2048]{2,1,0:T(2,128)(2,1)} %dual_hbm.1, bf16[4,2,2048]{2,1,0:T(2,128)(2,1)} %forw_hbm.1, bf16[4,2,2048]{2,1,0:T(2,128)(2,1)} %sino_hbm.1), custom_call_target="tpu_custom_call" | custom-call | tf_op jit(solution)/shard_map/pack_kernel/pallas_call | solution.py:313
  1.5 2.7 %collective-permute-start.1 = (bf16[12,2,2048]{2,1,0:T(2,128)(2,1)S(1)}, bf16[12,2,2048]{2,1,0:T(2,128)(2,1)S(1)}, u32[]{:S(2)}, u32[]{:S(2)}) collective-permute-start(bf16[12,2,2048]{2,1,0:T(2,128)(2,1)S(1)} %pack_kernel.1.own_ref), channel_id=1, source_target_pairs={{0,240},{16,32},{32,16},{48,64},{64,48},{80,96},{96,80},{112,128},... | collective-permute-start | bytes 294920 | tf_op jit(solution)/shard_map/ppermute | solution.py:324
  4.1 3.7 %collective-permute-start = (bf16[12,2,2048]{2,1,0:T(2,128)(2,1)S(1)}, bf16[12,2,2048]{2,1,0:T(2,128)(2,1)S(1)}, u32[]{:S(2)}, u32[]{:S(2)}) collective-permute-start(bf16[12,2,2048]{2,1,0:T(2,128)(2,1)S(1)} %pack_kernel.1.own_ref), channel_id=1, source_target_pairs={{0,16},{16,0},{32,48},{48,32},{64,80},{80,64},{96,112},{112,96},{1... | collective-permute-start | bytes 294920 | tf_op jit(solution)/shard_map/ppermute | solution.py:323
  7.9 1.5 %layout_kernel.1 = (bf16[512,256]{1,0:T(8,128)(2,1)S(1)}, bf16[576,256]{1,0:T(8,128)(2,1)S(1)}, f32[24,384]{1,0:T(8,128)S(1)}, f32[32,128]{1,0:T(8,128)S(1)}, f3...) custom-call(bf16[9,3,32]{2,1,0:T(4,128)(2,1)} %bitcast.13, bf16[9,32,32]{2,1,0:T(8,128)(2,1)} %bitcast.12, ...), custom_call_target="tpu_custom_call" | custom-call | tf_op jit(solution)/shard_map/layout_kernel/pallas_call | solution.py:326
  9.3 0.0 collective-permute-done.1.odd_ref
  9.4 0.0 collective-permute-done.even_ref
  9.4 8.7 %field_kernel.1 = (bf16[4,2,2048]{2,1,0:T(2,128)(2,1)}, f32[16,4,128]{2,1,0:T(4,128)S(1)}) custom-call(f32[4]{0:T(128)} %mag_hbm.1, f32[4]{0:T(128)} %move_hbm.1, f32[4]{0:T(128)} %frac_hbm.1, bf16[15,256,256]{2,1,0:T(8,128)(2,1)} %constant.13.ramp_hbm, bf16[12,2,2048]{2,1,0:T(2,128)(2,1)S(1)} %pack_kernel.1.own_ref, ...), custom_call_target="tpu_custom_call" | custom-call | tf_op jit(solution)/shard_map/field_kernel/pallas_call | solution.py:349
  18.0 14.5 %all_to_all.10 = f32[16,4,128]{2,1,0:T(4,128)S(1)} all-to-all(f32[16,4,128]{2,1,0:T(4,128)S(1)} %get-tuple-element.17), channel_id=1, replica_groups=mesh['ang'=16,'row'=16] {'ang'}, dimensions={0} | all-to-all | bytes 65536 | tf_op jit(solution)/shard_map/all_to_all | solution.py:373
  32.6 0.2 place_kernel.1
  32.7 16.7 %all_to_all.11 = f32[16,16,128]{2,1,0:T(8,128)S(1)} all-to-all(f32[16,16,128]{2,1,0:T(8,128)S(1)} %bitcast.10), channel_id=1, replica_groups=mesh['ang'=16,'row'=16] {'row'}, dimensions={0} | all-to-all | bytes 262144 | tf_op jit(solution)/shard_map/all_to_all | solution.py:382
  49.4 0.6 %broadcast_multiply_fusion = f32[16,128]{1,0:T(8,128)} fusion(f32[16,128]{1,0:T(8,128)S(1)} %reduce_sum.9), kind=kLoop, calls=%fused_computation | loop fusion | flops 2048 | bytes 16384 | tf_op jit(solution)/shard_map/mul | solution.py:383
  (1 shorter events, 0.0 us)
Async XLA Ops:
  1.5 7.9 %collective-permute-start.1 = (bf16[12,2,2048]{2,1,0:T(2,128)(2,1)S(1)}, bf16[12,2,2048]{2,1,0:T(2,128)(2,1)S(1)}, u32[]{:S(2)}, u32[]{:S(2)}) collective-permute-start(bf16[12,2,2048]{2,1,0:T(2,128)(2,1)S(1)} %pack_kernel.1.own_ref), channel_id=1, source_target_pairs={{0,240},{16,32},{32,16},{48,64},{64,48},{80,96},{96,80},{112,128},... | collective-permute-start | bytes 294920 | tf_op jit(solution)/shard_map/ppermute | solution.py:324
  4.1 5.2 %collective-permute-start = (bf16[12,2,2048]{2,1,0:T(2,128)(2,1)S(1)}, bf16[12,2,2048]{2,1,0:T(2,128)(2,1)S(1)}, u32[]{:S(2)}, u32[]{:S(2)}) collective-permute-start(bf16[12,2,2048]{2,1,0:T(2,128)(2,1)S(1)} %pack_kernel.1.own_ref), channel_id=1, source_target_pairs={{0,16},{16,0},{32,48},{48,32},{64,80},{80,64},{96,112},{112,96},{1... | collective-permute-start | bytes 294920 | tf_op jit(solution)/shard_map/ppermute | solution.py:323

commit v2 on v1

--- a/solution.py
+++ b/solution.py
@@ -109,8 +109,7 @@
         wide = base2[tap * CH:(tap + 1) * CH, :]
         for ang in range(SPAN - 4):
             rolled = pltpu.roll(wide, CH * ang, 1) if ang else wide
-            start = tap * HALF2 + ang * CH
-            w2_ref[start:start + CH, :] = rolled.astype(bf16)
+            w2_ref[ang * CH:(ang + 1) * CH, tap * HALF1:(tap + 1) * HALF1] = rolled.astype(bf16)
     base3[...] = jnp.zeros(base3.shape, f32)
     for ang_tap in range(3):
         base3[0:3, ang_tap * CH:(ang_tap + 1) * CH] = last_ref[ang_tap].astype(f32)
@@ -151,7 +150,7 @@
     mag_hbm, move_hbm, frac_hbm, ramp_hbm, own_ref, even_ref, odd_ref,
     w1_ref, w2_ref, w3_ref, col1_ref, col2_ref,
     dual_hbm, send_ref,
-    x32, xcat, act1, taps2, act2, ramp_ref, dual_ref, mag_ref, move_ref, frac_ref, sems,
+    x32, xcat, act1, act2, ramp_ref, dual_ref, mag_ref, move_ref, frac_ref, sems,
 ):
     f32, bf16 = jnp.float32, jnp.bfloat16
     loads = [
@@ -193,41 +192,32 @@
     xcat[192:256, :] = jnp.zeros((64, U), bf16)
 
     bias1 = col1_ref[:, 0:1]
-
-    def first_layer(step, carry):
-        cols = pl.ds(pl.multiple_of(step * BLK, BLK), BLK)
-        block = jnp.dot(w1_ref[...], xcat[:, cols], preferred_element_type=f32)
-        for part in range(ROWS1 // CH):
-            rows = slice(part * CH, (part + 1) * CH)
-            act1[rows, cols] = silu(block[rows] + bias1).astype(bf16)
-        return carry
-
-    lax.fori_loop(0, NBLK, first_layer, 0)
-
-    def second_dots(step, carry):
-        cols = pl.ds(pl.multiple_of(step * BLK, BLK), BLK)
-        for row in range(ROWS_DEV):
-            taps2[row, :, cols] = jnp.dot(
-                w2_ref[...], act1[row * HALF1:(row + 1) * HALF1, cols], preferred_element_type=f32
-            )
-        return carry
-
-    lax.fori_loop(0, NBLK, second_dots, 0)
-
     bias2 = col2_ref[:, 0:1]
-
-    def second_sum(step, carry):
-        start = pl.multiple_of(step * CH, CH)
-        for row in range(ROWS_DEV):
-            before = shifted(taps2[row, pl.ds(start, CH), :], -1)
-            here = taps2[row, pl.ds(HALF2 + start, CH), :]
-            after = shifted(taps2[row, pl.ds(2 * HALF2 + start, CH), :], 1)
-            total = before + here + after + bias2
-            act2[pl.ds(row * HALF2 + start, CH), :] = silu(total).astype(bf16)
-        return carry
-
-    lax.fori_loop(0, HALF2 // CH, second_sum, 0)
-
+    edge = lax.broadcasted_iota(jnp.int32, (HALF1, LANES), 1)
+    for row in range(ROWS_DEV):
+        for step in range(NBLK):
+            cols = slice(step * BLK, (step + 1) * BLK)
+            block = jnp.dot(w1_ref[row * HALF1:(row + 1) * HALF1, :], xcat[:, cols], preferred_element_type=f32)
+            for part in range(HALF1 // CH):
+                rows = slice(part * CH, (part + 1) * CH)
+                act1[row, HALF1 + part * CH:HALF1 + (part + 1) * CH, cols] = silu(block[rows] + bias1).astype(bf16)
+        here = act1[row, HALF1:2 * HALF1, :]
+        before = pltpu.roll(here, 1, 1)
+        after = pltpu.roll(here, U - 1, 1)
+        act1[row, 0:HALF1, LANES:] = before[:, LANES:]
+        act1[row, 0:HALF1, 0:LANES] = jnp.where(edge == 0, 0.0, before[:, 0:LANES].astype(f32)).astype(bf16)
+        act1[row, 2 * HALF1:, 0:U - LANES] = after[:, 0:U - LANES]
+        last = after[:, U - LANES:].astype(f32)
+        act1[row, 2 * HALF1:, U - LANES:] = jnp.where(edge == LANES - 1, 0.0, last).astype(bf16)
+    for row in range(ROWS_DEV):
+        for step in range(NBLK):
+            cols = slice(step * BLK, (step + 1) * BLK)
+            block = jnp.dot(w2_ref[...], act1[row, :, cols], preferred_element_type=f32)
+            for part in range(HALF2 // CH):
+                rows = slice(part * CH, (part + 1) * CH)
+                act2[row * HALF2 + part * CH:row * HALF2 + (part + 1) * CH, cols] = (
+                    silu(block[rows] + bias2).astype(bf16)
+                )
     taps3 = jnp.dot(w3_ref[...].astype(bf16), act2[...], preferred_element_type=f32)
     update = shifted(taps3[0:8], -1) + taps3[8:16] + shifted(taps3[16:24], 1)
     own_dual = x32[2 * HALO:2 * HALO + OUT8, :]
@@ -327,7 +317,7 @@
         layout_kernel,
         out_shape=(
             jax.ShapeDtypeStruct((ROWS1, 256), bf16),
-            jax.ShapeDtypeStruct((3 * HALF2, HALF1), bf16),
+            jax.ShapeDtypeStruct((HALF2, 3 * HALF1), bf16),
             jax.ShapeDtypeStruct((24, 2 * HALF2), f32),
             jax.ShapeDtypeStruct((CH, LANES), f32),
             jax.ShapeDtypeStruct((CH, LANES), f32),
@@ -357,8 +347,7 @@
         scratch_shapes=[
             pltpu.VMEM((64, U), f32),
             pltpu.VMEM((256, U), bf16),
-            pltpu.VMEM((ROWS1, U), bf16),
-            pltpu.VMEM((ROWS_DEV, 3 * HALF2, U), f32),
+            pltpu.VMEM((ROWS_DEV, 3 * HALF1, U), bf16),
             pltpu.VMEM((2 * HALF2, U), bf16),
             pltpu.VMEM((2 * NBLK - 1, BLK, BLK), bf16),
             pltpu.VMEM((ANG_DEV, ROWS_DEV, U), bf16),

time: 50.3 us -> 45.9 us (0.913)
  Pallas kernels: 11.1 us -> 6.67 us
    pallas_call x1, Pallas kernels: 8.66 us -> 4.24 us  [per_device(): pl.pallas_call(field_kernel, out_shape=(jax.ShapeDtypeStruct((ANG_DEV, RO...]
where the time goes in v2:
time: 45.9 us; the launch traced here: 45.6 us
  blocking collectives  31.2 us (68%)
  Pallas kernels  6.67 us (15%)
  starting transfers between devices  6.42 us (14%)
  between operations  0.68 us (1%)
  other arithmetic  0.62 us (1%)
    all_to_all x1, blocking collectives, per_device(): lax.all_to_all(placed.reshape(ROW_DEVS, SLABS_DEV * SLAB_Z, LANES), 'row'...  16.7 us
    all_to_all x1, blocking collectives, per_device(): got = lax.all_to_all(send, 'ang', 0, 0, tiled=True)  14.5 us
    pallas_call x1, Pallas kernels, per_device(): pl.pallas_call(field_kernel, out_shape=(jax.ShapeDtypeStruct((ANG_DEV, RO...  4.24 us
    ppermute x1, starting transfers between devices, per_device(): even = lax.ppermute(own, 'ang', [(i, i ^ 1) for i in range(count)])  3.73 us
    ppermute x1, starting transfers between devices, per_device(): lax.ppermute(own, 'ang', [(i, (i + 1 if i % 2 else i - 1) % count) for i...  2.69 us
    pallas_call x1, Pallas kernels, per_device(): pl.pallas_call(layout_kernel, out_shape=(jax.ShapeDtypeStruct((ROWS1, 256...  1.46 us
  transfers between devices with their start and end apart: 2, of which 0 were waited for; matrix products, arithmetic and copies ran while one was open for 0% of the time, Pallas kernels for 3%

profile of v2, /device:TPU:1, one launch (start us, length us, event | category | flops | bytes accessed | tf_op | source)
XLA Modules:
  0.0 45.6 jit_solution(6605371760235535892)
XLA Ops:
  0.6 0.8 %pack_kernel.1.own_ref = bf16[12,2,2048]{2,1,0:T(2,128)(2,1)S(1)} custom-call(bf16[4,2,2048]{2,1,0:T(2,128)(2,1)} %dual_hbm.1, bf16[4,2,2048]{2,1,0:T(2,128)(2,1)} %forw_hbm.1, bf16[4,2,2048]{2,1,0:T(2,128)(2,1)} %sino_hbm.1), custom_call_target="tpu_custom_call" | custom-call | tf_op jit(solution)/shard_map/pack_kernel/pallas_call | solution.py:303
  1.5 2.7 %collective-permute-start.1 = (bf16[12,2,2048]{2,1,0:T(2,128)(2,1)S(1)}, bf16[12,2,2048]{2,1,0:T(2,128)(2,1)S(1)}, u32[]{:S(2)}, u32[]{:S(2)}) collective-permute-start(bf16[12,2,2048]{2,1,0:T(2,128)(2,1)S(1)} %pack_kernel.1.own_ref), channel_id=1, source_target_pairs={{0,240},{16,32},{32,16},{48,64},{64,48},{80,96},{96,80},{112,128},... | collective-permute-start | bytes 294920 | tf_op jit(solution)/shard_map/ppermute | solution.py:314
  4.1 3.7 %collective-permute-start = (bf16[12,2,2048]{2,1,0:T(2,128)(2,1)S(1)}, bf16[12,2,2048]{2,1,0:T(2,128)(2,1)S(1)}, u32[]{:S(2)}, u32[]{:S(2)}) collective-permute-start(bf16[12,2,2048]{2,1,0:T(2,128)(2,1)S(1)} %pack_kernel.1.own_ref), channel_id=1, source_target_pairs={{0,16},{16,0},{32,48},{48,32},{64,80},{80,64},{96,112},{112,96},{1... | collective-permute-start | bytes 294920 | tf_op jit(solution)/shard_map/ppermute | solution.py:313
  7.9 1.5 %layout_kernel.1 = (bf16[512,256]{1,0:T(8,128)(2,1)S(1)}, bf16[192,768]{1,0:T(8,128)(2,1)S(1)}, f32[24,384]{1,0:T(8,128)S(1)}, f32[32,128]{1,0:T(8,128)S(1)}, f3...) custom-call(bf16[9,3,32]{2,1,0:T(4,128)(2,1)} %bitcast.13, bf16[9,32,32]{2,1,0:T(8,128)(2,1)} %bitcast.12, ...), custom_call_target="tpu_custom_call" | custom-call | tf_op jit(solution)/shard_map/layout_kernel/pallas_call | solution.py:316
  9.3 0.0 collective-permute-done.1.odd_ref
  9.4 0.0 collective-permute-done.even_ref
  9.4 4.2 %field_kernel.1 = (bf16[4,2,2048]{2,1,0:T(2,128)(2,1)}, f32[16,4,128]{2,1,0:T(4,128)S(1)}) custom-call(f32[4]{0:T(128)} %mag_hbm.1, f32[4]{0:T(128)} %move_hbm.1, f32[4]{0:T(128)} %frac_hbm.1, bf16[15,256,256]{2,1,0:T(8,128)(2,1)} %constant.13.ramp_hbm, bf16[12,2,2048]{2,1,0:T(2,128)(2,1)S(1)} %pack_kernel.1.own_ref, ...), custom_call_target="tpu_custom_call" | custom-call | tf_op jit(solution)/shard_map/field_kernel/pallas_call | solution.py:339
  13.6 14.5 %all_to_all.10 = f32[16,4,128]{2,1,0:T(4,128)S(1)} all-to-all(f32[16,4,128]{2,1,0:T(4,128)S(1)} %get-tuple-element.17), channel_id=1, replica_groups=mesh['ang'=16,'row'=16] {'ang'}, dimensions={0} | all-to-all | bytes 65536 | tf_op jit(solution)/shard_map/all_to_all | solution.py:362
  28.2 0.2 place_kernel.1
  28.3 16.7 %all_to_all.11 = f32[16,16,128]{2,1,0:T(8,128)S(1)} all-to-all(f32[16,16,128]{2,1,0:T(8,128)S(1)} %bitcast.10), channel_id=1, replica_groups=mesh['ang'=16,'row'=16] {'row'}, dimensions={0} | all-to-all | bytes 262144 | tf_op jit(solution)/shard_map/all_to_all | solution.py:371
  45.0 0.6 %broadcast_multiply_fusion = f32[16,128]{1,0:T(8,128)} fusion(f32[16,128]{1,0:T(8,128)S(1)} %reduce_sum.9), kind=kLoop, calls=%fused_computation | loop fusion | flops 2048 | bytes 16384 | tf_op jit(solution)/shard_map/mul | solution.py:372
  (1 shorter events, 0.0 us)
Async XLA Ops:
  1.5 7.9 %collective-permute-start.1 = (bf16[12,2,2048]{2,1,0:T(2,128)(2,1)S(1)}, bf16[12,2,2048]{2,1,0:T(2,128)(2,1)S(1)}, u32[]{:S(2)}, u32[]{:S(2)}) collective-permute-start(bf16[12,2,2048]{2,1,0:T(2,128)(2,1)S(1)} %pack_kernel.1.own_ref), channel_id=1, source_target_pairs={{0,240},{16,32},{32,16},{48,64},{64,48},{80,96},{96,80},{112,128},... | collective-permute-start | bytes 294920 | tf_op jit(solution)/shard_map/ppermute | solution.py:314
  4.1 5.2 %collective-permute-start = (bf16[12,2,2048]{2,1,0:T(2,128)(2,1)S(1)}, bf16[12,2,2048]{2,1,0:T(2,128)(2,1)S(1)}, u32[]{:S(2)}, u32[]{:S(2)}) collective-permute-start(bf16[12,2,2048]{2,1,0:T(2,128)(2,1)S(1)} %pack_kernel.1.own_ref), channel_id=1, source_target_pairs={{0,16},{16,0},{32,48},{48,32},{64,80},{80,64},{96,112},{112,96},{1... | collective-permute-start | bytes 294920 | tf_op jit(solution)/shard_map/ppermute | solution.py:313

commit v3 on v2

--- a/solution.py
+++ b/solution.py
@@ -25,7 +25,8 @@
 SPAN = ANG_DEV + 2 * HALO
 ROWS1 = ROWS_DEV * (SPAN - 2) * CH
 HALF1 = (SPAN - 2) * CH
-HALF2 = (SPAN - 4) * CH
+GROUP1 = 5 * CH
+GROUP2 = 3 * CH
 OUT8 = ANG_DEV * ROWS_DEV
 CENTRE = (U - 1) / 2.0
 MIB = 1024 * 1024
@@ -67,11 +68,20 @@
     return max(low, 0) // LANES, min(high, U - 1) // LANES
 
 
-def pack_kernel(dual_hbm, forw_hbm, sino_hbm, out_ref, sems):
-    loads = [
-        pltpu.make_async_copy(field, out_ref.at[pl.ds(at * ANG_DEV, ANG_DEV)], sems.at[at])
-        for at, field in enumerate((dual_hbm, forw_hbm, sino_hbm))
-    ]
+def parity():
+    return lax.axis_index("ang") % 2
+
+
+def turned(index, last):
+    return index + parity() * (last - 2 * index)
+
+
+def pack_kernel(dual_hbm, forw_hbm, sino_hbm, own_ref, far_ref, sems):
+    loads = []
+    for at, field in enumerate((dual_hbm, forw_hbm, sino_hbm)):
+        side = field.at[pl.ds(parity(), HALO)]
+        loads.append(pltpu.make_async_copy(side, far_ref.at[pl.ds(at * HALO, HALO)], sems.at[at]))
+        loads.append(pltpu.make_async_copy(field, own_ref.at[pl.ds(at * ANG_DEV, ANG_DEV)], sems.at[3 + at]))
     for load in loads:
         load.start()
     for load in loads:
@@ -81,12 +91,14 @@
 def layout_kernel(
     first_ref, middle_ref, last_ref, bias1_ref, bias2_ref, order_ref, offs_ref,
     w1_ref, w2_ref, w3_ref, col1_ref, col2_ref, pick_ref,
-    gather1, base2, base3,
+    gather1, base2,
 ):
     f32, bf16 = jnp.float32, jnp.bfloat16
     gather1[...] = jnp.zeros(gather1.shape, f32)
-    for part in range(9):
-        gather1[3 * part:3 * part + 3, 0:CH] = first_ref[part].astype(f32)
+    for ang_tap in range(3):
+        for tap in range(3):
+            part = 3 * ang_tap + tap
+            gather1[3 * part:3 * part + 3, 0:CH] = first_ref[3 * turned(ang_tap, 2) + tap].astype(f32)
     key = lax.broadcasted_iota(jnp.int32, (32, 256), 0)
     lane = lax.broadcasted_iota(jnp.int32, (32, 256), 1)
     wanted = (key // 3 % 3) * 64 + (key % 3) * (2 * SPAN) + (key // 9) * 2
@@ -103,24 +115,21 @@
     base2[...] = jnp.zeros(base2.shape, f32)
     for ang_tap in range(3):
         for tap in range(3):
-            block = middle_ref[3 * ang_tap + tap].astype(f32)
-            base2[tap * CH:(tap + 1) * CH, ang_tap * CH:(ang_tap + 1) * CH] = block
-    for tap in range(3):
-        wide = base2[tap * CH:(tap + 1) * CH, :]
-        for ang in range(SPAN - 4):
-            rolled = pltpu.roll(wide, CH * ang, 1) if ang else wide
-            w2_ref[ang * CH:(ang + 1) * CH, tap * HALF1:(tap + 1) * HALF1] = rolled.astype(bf16)
-    base3[...] = jnp.zeros(base3.shape, f32)
+            block = middle_ref[3 * turned(ang_tap, 2) + tap].astype(f32)
+            for ang in range(3):
+                start = tap * GROUP1 + (ang + ang_tap) * CH
+                base2[ang * CH:(ang + 1) * CH, start:start + CH] = block
+    w2_ref[...] = base2[...].astype(bf16)
+    w3_ref[...] = jnp.zeros(w3_ref.shape, f32)
     for ang_tap in range(3):
-        base3[0:3, ang_tap * CH:(ang_tap + 1) * CH] = last_ref[ang_tap].astype(f32)
-    wide = base3[...]
-    for ang in range(ANG_DEV):
-        for row in range(ROWS_DEV):
-            shift = CH * ang + HALF2 * row
-            rolled = pltpu.roll(wide, shift, 1) if shift else wide
-            for tap in range(3):
-                at = tap * OUT8 + ang * ROWS_DEV + row
-                w3_ref[at:at + 1, :] = rolled[tap:tap + 1, :]
+        block = last_ref[turned(ang_tap, 2)].astype(f32)
+        for ang in range(ANG_DEV):
+            source = ang + ang_tap
+            for row in range(ROWS_DEV):
+                start = row * GROUP2 + source % 3 * CH
+                for tap in range(3):
+                    at = tap * OUT8 + ang * ROWS_DEV + row
+                    w3_ref[source // 3, at:at + 1, start:start + CH] = block[tap:tap + 1, :]
     square = (CH, CH)
     eye = lax.broadcasted_iota(jnp.int32, square, 0) == lax.broadcasted_iota(jnp.int32, square, 1)
     for bias_ref, col_ref in ((bias1_ref, col1_ref), (bias2_ref, col2_ref)):
@@ -146,85 +155,130 @@
     pick_ref[...] = jnp.where(starts + offset.astype(f32) == 0.0, 1.0, 0.0).astype(bf16)
 
 
-def field_kernel(
-    mag_hbm, move_hbm, frac_hbm, ramp_hbm, own_ref, even_ref, odd_ref,
-    w1_ref, w2_ref, w3_ref, col1_ref, col2_ref,
-    dual_hbm, send_ref,
-    x32, xcat, act1, act2, ramp_ref, dual_ref, mag_ref, move_ref, frac_ref, sems,
-):
-    f32, bf16 = jnp.float32, jnp.bfloat16
-    loads = [
-        pltpu.make_async_copy(mag_hbm, mag_ref, sems.at[0]),
-        pltpu.make_async_copy(move_hbm, move_ref, sems.at[1]),
-        pltpu.make_async_copy(frac_hbm, frac_ref, sems.at[2]),
-        pltpu.make_async_copy(ramp_hbm, ramp_ref, sems.at[3]),
-    ]
-    for load in loads:
-        load.start()
-    x32[3 * 2 * SPAN:64, :] = jnp.zeros((64 - 3 * 2 * SPAN, U), f32)
-
-    def lay(left_ref, right_ref):
-        for field in range(FIELDS):
-            base = field * 2 * SPAN
-            for ang in range(HALO):
-                x32[base + 2 * ang:base + 2 * ang + 2, :] = left_ref[field * ANG_DEV + 1 + ang].astype(f32)
-                at = base + 2 * (HALO + ANG_DEV + ang)
-                x32[at:at + 2, :] = right_ref[field * ANG_DEV + ang].astype(f32)
-
+def lay_inputs(x32, xcat, own_ref, side_ref, side, sent):
+    f32, bf16 = jnp.float32, jnp.bfloat16
+    x32[...] = jnp.zeros(x32.shape, f32)
     for field in range(FIELDS):
+        base = field * 2 * SPAN
         for ang in range(ANG_DEV):
-            at = field * 2 * SPAN + 2 * (HALO + ang)
-            x32[at:at + 2, :] = own_ref[field * ANG_DEV + ang].astype(f32)
-    parity = lax.axis_index("ang") % 2
-
-    @pl.when(parity == 0)
-    def _():
-        lay(odd_ref, even_ref)
-
-    @pl.when(parity == 1)
-    def _():
-        lay(even_ref, odd_ref)
-
+            at = base + 2 * (HALO + ang)
+            x32[at:at + 2, :] = own_ref[field * ANG_DEV + turned(ang, ANG_DEV - 1)].astype(f32)
+        for ang in range(HALO):
+            at = base + 2 * (side + ang)
+            x32[at:at + 2, :] = side_ref[field * sent + turned(ang, sent - 1)].astype(f32)
     stacked = x32[...]
     xcat[0:64, :] = shifted(stacked, -1).astype(bf16)
     xcat[64:128, :] = stacked.astype(bf16)
     xcat[128:192, :] = shifted(stacked, 1).astype(bf16)
     xcat[192:256, :] = jnp.zeros((64, U), bf16)
 
-    bias1 = col1_ref[:, 0:1]
-    bias2 = col2_ref[:, 0:1]
-    edge = lax.broadcasted_iota(jnp.int32, (HALF1, LANES), 1)
-    for row in range(ROWS_DEV):
-        for step in range(NBLK):
-            cols = slice(step * BLK, (step + 1) * BLK)
-            block = jnp.dot(w1_ref[row * HALF1:(row + 1) * HALF1, :], xcat[:, cols], preferred_element_type=f32)
-            for part in range(HALF1 // CH):
-                rows = slice(part * CH, (part + 1) * CH)
-                act1[row, HALF1 + part * CH:HALF1 + (part + 1) * CH, cols] = silu(block[rows] + bias1).astype(bf16)
-        here = act1[row, HALF1:2 * HALF1, :]
+
+def first_layer(xcat, w1_ref, bias1, act1, row, first, count):
+    f32, bf16 = jnp.float32, jnp.bfloat16
+    start, size = row * HALF1 + first * CH, count * CH
+    lane = lax.broadcasted_iota(jnp.int32, (size, LANES), 1)
+    nothing = jnp.zeros((size, LANES), bf16)
+    before_edge, after_rest = nothing, None
+    for step in range(NBLK):
+        cols = slice(step * BLK, (step + 1) * BLK)
+        block = jnp.dot(w1_ref[start:start + size, :], xcat[:, cols], preferred_element_type=f32)
+        act = jnp.concatenate(
+            [silu(block[part * CH:(part + 1) * CH] + bias1) for part in range(count)], axis=0
+        ).astype(bf16)
+        act1[row, GROUP1:GROUP1 + size, cols] = act
+        before = pltpu.roll(act, 1, 1)
+        act1[row, 0:size, step * BLK:step * BLK + LANES] = jnp.where(lane == 0, before_edge, before[:, 0:LANES])
+        act1[row, 0:size, step * BLK + LANES:(step + 1) * BLK] = before[:, LANES:]
+        before_edge = before[:, 0:LANES]
+        after = pltpu.roll(act, BLK - 1, 1)
+        act1[row, 2 * GROUP1:2 * GROUP1 + size, step * BLK:step * BLK + LANES] = after[:, 0:LANES]
+        if step:
+            act1[row, 2 * GROUP1:2 * GROUP1 + size, step * BLK - LANES:step * BLK] = jnp.where(
+                lane == LANES - 1, after[:, LANES:], after_rest
+            )
+        after_rest = after[:, LANES:]
+    act1[row, 2 * GROUP1:2 * GROUP1 + size, U - LANES:] = jnp.where(lane == LANES - 1, nothing, after_rest)
+
+
+def first_layer_whole(xcat, w1_ref, bias1, act1, row, first, count):
+    f32, bf16 = jnp.float32, jnp.bfloat16
+    start = row * HALF1 + first * CH
+    for step in range(NBLK):
+        cols = slice(step * BLK, (step + 1) * BLK)
+        block = jnp.dot(w1_ref[start:start + count * CH, :], xcat[:, cols], preferred_element_type=f32)
+        for part in range(count):
+            rows = slice(GROUP1 + part * CH, GROUP1 + (part + 1) * CH)
+            act1[row, rows, cols] = silu(block[part * CH:(part + 1) * CH] + bias1).astype(bf16)
+    edge = lax.broadcasted_iota(jnp.int32, (CH, LANES), 1)
+    for part in range(count):
+        low, middle, high = (slice(tap * GROUP1 + part * CH, tap * GROUP1 + (part + 1) * CH) for tap in range(3))
+        here = act1[row, middle, :]
         before = pltpu.roll(here, 1, 1)
         after = pltpu.roll(here, U - 1, 1)
-        act1[row, 0:HALF1, LANES:] = before[:, LANES:]
-        act1[row, 0:HALF1, 0:LANES] = jnp.where(edge == 0, 0.0, before[:, 0:LANES].astype(f32)).astype(bf16)
-        act1[row, 2 * HALF1:, 0:U - LANES] = after[:, 0:U - LANES]
+        act1[row, low, LANES:] = before[:, LANES:]
+        act1[row, low, 0:LANES] = jnp.where(edge == 0, 0.0, before[:, 0:LANES].astype(f32)).astype(bf16)
+        act1[row, high, 0:U - LANES] = after[:, 0:U - LANES]
         last = after[:, U - LANES:].astype(f32)
-        act1[row, 2 * HALF1:, U - LANES:] = jnp.where(edge == LANES - 1, 0.0, last).astype(bf16)
+        act1[row, high, U - LANES:] = jnp.where(edge == LANES - 1, 0.0, last).astype(bf16)
+
+
+def second_layer(w2_ref, bias2, act1, act2):
+    f32, bf16 = jnp.float32, jnp.bfloat16
     for row in range(ROWS_DEV):
         for step in range(NBLK):
             cols = slice(step * BLK, (step + 1) * BLK)
             block = jnp.dot(w2_ref[...], act1[row, :, cols], preferred_element_type=f32)
-            for part in range(HALF2 // CH):
-                rows = slice(part * CH, (part + 1) * CH)
-                act2[row * HALF2 + part * CH:row * HALF2 + (part + 1) * CH, cols] = (
-                    silu(block[rows] + bias2).astype(bf16)
-                )
-    taps3 = jnp.dot(w3_ref[...].astype(bf16), act2[...], preferred_element_type=f32)
+            for part in range(3):
+                rows = slice(row * GROUP2 + part * CH, row * GROUP2 + (part + 1) * CH)
+                act2[rows, cols] = silu(block[part * CH:(part + 1) * CH] + bias2).astype(bf16)
+
+
+def near_kernel(
+    ramp_hbm, own_ref, near_ref, w1_ref, w2_ref, w3_ref, col1_ref, col2_ref,
+    shared_ref, taps_ref, ramp_ref,
+    x32, xcat, act1, act2, sem,
+):
+    load = pltpu.make_async_copy(ramp_hbm, ramp_ref, sem)
+    load.start()
+    bias1, bias2 = col1_ref[:, 0:1], col2_ref[:, 0:1]
+    lay_inputs(x32, xcat, own_ref, near_ref, HALO + ANG_DEV, ANG_DEV)
+    for row in range(ROWS_DEV):
+        first_layer_whole(xcat, w1_ref, bias1, act1, row, 3, 5)
+        for tap in range(3):
+            shared_ref[row, tap] = act1[row, tap * GROUP1:tap * GROUP1 + 2 * CH, :]
+    second_layer(w2_ref, bias2, act1, act2)
+    taps_ref[...] = jnp.dot(w3_ref[1].astype(jnp.bfloat16), act2[...], preferred_element_type=jnp.float32)
+    load.wait()
+
+
+def far_kernel(
+    mag_hbm, move_hbm, frac_hbm, own_ref, far_ref, shared_ref, taps_ref, ramp_ref,
+    w1_ref, w2_ref, w3_ref, col1_ref, col2_ref,
+    dual_hbm, send_ref,
+    x32, xcat, act1, act2, dual_ref, mag_ref, move_ref, frac_ref, sems,
+):
+    f32, bf16 = jnp.float32, jnp.bfloat16
+    loads = [
+        pltpu.make_async_copy(mag_hbm, mag_ref, sems.at[0]),
+        pltpu.make_async_copy(move_hbm, move_ref, sems.at[1]),
+        pltpu.make_async_copy(frac_hbm, frac_ref, sems.at[2]),
+    ]
+    for load in loads:
+        load.start()
+    bias1, bias2 = col1_ref[:, 0:1], col2_ref[:, 0:1]
+    lay_inputs(x32, xcat, own_ref, far_ref, 0, HALO)
+    for row in range(ROWS_DEV):
+        first_layer(xcat, w1_ref, bias1, act1, row, 0, 3)
+        for tap in range(3):
+            act1[row, tap * GROUP1 + 3 * CH:(tap + 1) * GROUP1, :] = shared_ref[row, tap]
+    second_layer(w2_ref, bias2, act1, act2)
+    taps3 = taps_ref[...] + jnp.dot(w3_ref[0].astype(bf16), act2[...], preferred_element_type=f32)
     update = shifted(taps3[0:8], -1) + taps3[8:16] + shifted(taps3[16:24], 1)
     own_dual = x32[2 * HALO:2 * HALO + OUT8, :]
     new_dual = (own_dual + update).astype(bf16)
     for ang in range(ANG_DEV):
-        dual_ref[ang] = new_dual[2 * ang:2 * ang + 2, :]
-    store = pltpu.make_async_copy(dual_ref, dual_hbm, sems.at[4])
+        dual_ref[turned(ang, ANG_DEV - 1)] = new_dual[2 * ang:2 * ang + 2, :]
+    store = pltpu.make_async_copy(dual_ref, dual_hbm, sems.at[3])
     store.start()
     for load in loads:
         load.wait()
@@ -244,9 +298,9 @@
     ang_id = row_id // ROWS_DEV
 
     def per_angle(ref):
-        value = jnp.full((OUT8, LANES), ref[0], f32)
+        value = jnp.full((OUT8, LANES), ref[turned(0, ANG_DEV - 1)], f32)
         for ang in range(1, ANG_DEV):
-            value = jnp.where(ang_id == ang, ref[ang], value)
+            value = jnp.where(ang_id == ang, ref[turned(ang, ANG_DEV - 1)], value)
         return value
 
     mag, move, frac = per_angle(mag_ref), per_angle(move_ref), per_angle(frac_ref)
@@ -300,25 +354,28 @@
     f32, bf16 = jnp.float32, jnp.bfloat16
     vmem = pl.BlockSpec(memory_space=pltpu.VMEM)
     hbm = pl.BlockSpec(memory_space=pltpu.HBM)
-    own = pl.pallas_call(
+    own, far = pl.pallas_call(
         pack_kernel,
-        out_shape=jax.ShapeDtypeStruct((FIELDS * ANG_DEV, ROWS_DEV, U), bf16),
+        out_shape=(
+            jax.ShapeDtypeStruct((FIELDS * ANG_DEV, ROWS_DEV, U), bf16),
+            jax.ShapeDtypeStruct((FIELDS * HALO, ROWS_DEV, U), bf16),
+        ),
         in_specs=[hbm] * 3,
-        out_specs=vmem,
-        scratch_shapes=[pltpu.SemaphoreType.DMA((3,))],
+        out_specs=(vmem,) * 2,
+        scratch_shapes=[pltpu.SemaphoreType.DMA((6,))],
         compiler_params=pltpu.CompilerParams(vmem_limit_bytes=2 * MIB),
         name="pack_kernel",
     )(*map(in_hbm, (dual_field, forward, sinogram)))
     count = lax.axis_size("ang")
-    even = lax.ppermute(own, "ang", [(i, i ^ 1) for i in range(count)])
-    odd = lax.ppermute(own, "ang", [(i, (i + 1 if i % 2 else i - 1) % count) for i in range(count)])
+    near = lax.ppermute(own, "ang", [(i, i ^ 1) for i in range(count)])
+    far = lax.ppermute(far, "ang", [(i, (i + 1 if i % 2 else i - 1) % count) for i in range(count)])
     width = 3 * 4 * BLOCKS
     w1, w2, w3, col1, col2, pick = pl.pallas_call(
         layout_kernel,
         out_shape=(
             jax.ShapeDtypeStruct((ROWS1, 256), bf16),
-            jax.ShapeDtypeStruct((HALF2, 3 * HALF1), bf16),
-            jax.ShapeDtypeStruct((24, 2 * HALF2), f32),
+            jax.ShapeDtypeStruct((GROUP2, 3 * GROUP1), bf16),
+            jax.ShapeDtypeStruct((2, 24, 2 * GROUP2), f32),
             jax.ShapeDtypeStruct((CH, LANES), f32),
             jax.ShapeDtypeStruct((CH, LANES), f32),
             jax.ShapeDtypeStruct((SLABS_DEV * ROW_DEVS * SLAB_Z, width), bf16),
@@ -326,8 +383,7 @@
         out_specs=(vmem,) * 6,
         scratch_shapes=[
             pltpu.VMEM((32, LANES), f32),
-            pltpu.VMEM((3 * CH, HALF1), f32),
-            pltpu.VMEM((8, 2 * HALF2), f32),
+            pltpu.VMEM((GROUP2, 3 * GROUP1), f32),
         ],
         compiler_params=pltpu.CompilerParams(vmem_limit_bytes=8 * MIB),
         name="layout_kernel",
@@ -336,29 +392,46 @@
         last_weight.transpose(0, 2, 1, 3).reshape(3, 3, CH), first_bias[None], middle_bias[None],
         slab_order[None], offsets,
     )))
+    work = [
+        pltpu.VMEM((64, U), f32),
+        pltpu.VMEM((256, U), bf16),
+        pltpu.VMEM((ROWS_DEV, 3 * GROUP1, U), bf16),
+        pltpu.VMEM((ROWS_DEV * GROUP2, U), bf16),
+    ]
+    shared, taps, ramp = pl.pallas_call(
+        near_kernel,
+        out_shape=(
+            jax.ShapeDtypeStruct((ROWS_DEV, 3, 2 * CH, U), bf16),
+            jax.ShapeDtypeStruct((24, U), f32),
+            jax.ShapeDtypeStruct((2 * NBLK - 1, BLK, BLK), bf16),
+        ),
+        in_specs=[hbm] + [vmem] * 7,
+        out_specs=(vmem,) * 3,
+        scratch_shapes=work + [pltpu.SemaphoreType.DMA],
+        compiler_params=pltpu.CompilerParams(vmem_limit_bytes=24 * MIB),
+        name="near_kernel",
+    )(in_hbm(ramp_tiles()), own, near, w1, w2, w3, col1, col2)
     new_dual, send = pl.pallas_call(
-        field_kernel,
+        far_kernel,
         out_shape=(
             jax.ShapeDtypeStruct((ANG_DEV, ROWS_DEV, U), bf16),
             jax.ShapeDtypeStruct((BLOCKS, 4, LANES), f32),
         ),
-        in_specs=[hbm] * 4 + [vmem] * 8,
+        in_specs=[hbm] * 3 + [vmem] * 10,
         out_specs=(hbm, vmem),
-        scratch_shapes=[
-            pltpu.VMEM((64, U), f32),
-            pltpu.VMEM((256, U), bf16),
-            pltpu.VMEM((ROWS_DEV, 3 * HALF1, U), bf16),
-            pltpu.VMEM((2 * HALF2, U), bf16),
-            pltpu.VMEM((2 * NBLK - 1, BLK, BLK), bf16),
+        scratch_shapes=work + [
             pltpu.VMEM((ANG_DEV, ROWS_DEV, U), bf16),
             pltpu.SMEM((ANG_DEV,), f32),
             pltpu.SMEM((ANG_DEV,), f32),
             pltpu.SMEM((ANG_DEV,), f32),
-            pltpu.SemaphoreType.DMA((5,)),
+            pltpu.SemaphoreType.DMA((4,)),
         ],
-        compiler_params=pltpu.CompilerParams(vmem_limit_bytes=32 * MIB),
-        name="field_kernel",
-    )(*map(in_hbm, (magnify, detector_shift, row_fraction, ramp_tiles())), own, even, odd, w1, w2, w3, col1, col2)
+        compiler_params=pltpu.CompilerParams(vmem_limit_bytes=24 * MIB),
+        name="far_kernel",
+    )(
+        *map(in_hbm, (magnify, detector_shift, row_fraction)),
+        own, far, shared, taps, ramp, w1, w2, w3, col1, col2,
+    )
     got = lax.all_to_all(send, "ang", 0, 0, tiled=True)
     placed = pl.pallas_call(
         place_kernel,

time: 45.9 us -> 44.8 us (0.976)
  starting transfers between devices: 6.42 us -> 3.33 us
  blocking collectives: 31.2 us -> 32.4 us
  Pallas kernels: 6.67 us -> 7.37 us
    ppermute x2, starting transfers between devices: 6.42 us -> 3.33 us  [the longest x1 3.33 us: per_device(): near = lax.ppermute(own, 'ang', [(i, i ^ 1) for i in range(count)])]
    all_to_all x1, blocking collectives: 14.5 us -> 15.8 us  [per_device(): got = lax.all_to_all(send, 'ang', 0, 0, tiled=True)]
    pallas_call x2 -> x3, Pallas kernels: 5.05 us -> 5.77 us  [the longest x1 2.66 us: per_device(): pl.pallas_call(far_kernel, out_shape=(jax.ShapeDtypeStruct((ANG_DEV, ROWS...]
  transfers between devices with their start and end apart: 2 -> 2, of which waited for: 0 -> 1; matrix products, arithmetic and copies ran while one was open for 0% -> 0% of each run, Pallas kernels for 3% -> 8%
where the time goes in v3:
time: 44.8 us; the launch traced here: 44.6 us
  blocking collectives  32.4 us (72%)
  Pallas kernels  7.37 us (16%)
  starting transfers between devices  3.33 us (7%)
  between operations  0.68 us (2%)
  other arithmetic  0.62 us (1%)
    all_to_all x1, blocking collectives, per_device(): lax.all_to_all(placed.reshape(ROW_DEVS, SLABS_DEV * SLAB_Z, LANES), 'row'...  16.7 us
    all_to_all x1, blocking collectives, per_device(): got = lax.all_to_all(send, 'ang', 0, 0, tiled=True)  15.8 us
    ppermute x1, starting transfers between devices, per_device(): near = lax.ppermute(own, 'ang', [(i, i ^ 1) for i in range(count)])  3.33 us
    pallas_call x1, Pallas kernels, per_device(): pl.pallas_call(far_kernel, out_shape=(jax.ShapeDtypeStruct((ANG_DEV, ROWS...  2.66 us
    pallas_call x1, Pallas kernels, per_device(): pl.pallas_call(near_kernel, out_shape=(jax.ShapeDtypeStruct((ROWS_DEV, 3,...  2.21 us
    pallas_call x1, Pallas kernels, per_device(): pl.pallas_call(layout_kernel, out_shape=(jax.ShapeDtypeStruct((ROWS1, 256...  1.44 us
    pallas_call x1, Pallas kernels, per_device(): pl.pallas_call(pack_kernel, out_shape=(jax.ShapeDtypeStruct((FIELDS * ANG...  0.91 us
  transfers between devices with their start and end apart: 2, of which 1 were waited for; matrix products, arithmetic and copies ran while one was open for 0% of the time, Pallas kernels for 8%

profile of v3, /device:TPU:1, one launch (start us, length us, event | category | flops | bytes accessed | tf_op | source)
XLA Modules:
  0.0 44.6 jit_solution(7172893817905995690)
XLA Ops:
  0.6 0.9 %pack_kernel.1 = (bf16[12,2,2048]{2,1,0:T(2,128)(2,1)S(1)}, bf16[9,2,2048]{2,1,0:T(2,128)(2,1)S(1)}) custom-call(bf16[4,2,2048]{2,1,0:T(2,128)(2,1)} %dual_hbm.1, bf16[4,2,2048]{2,1,0:T(2,128)(2,1)} %forw_hbm.1, bf16[4,2,2048]{2,1,0:T(2,128)(2,1)} %sino_hbm.1), custom_call_target="tpu_custom_call" | custom-call | tf_op jit(solution)/shard_map/pack_kernel/pallas_call | solution.py:357
  1.5 3.3 %collective-permute-start.1 = (bf16[12,2,2048]{2,1,0:T(2,128)(2,1)S(1)}, bf16[12,2,2048]{2,1,0:T(2,128)(2,1)S(1)}, u32[]{:S(2)}, u32[]{:S(2)}) collective-permute-start(bf16[12,2,2048]{2,1,0:T(2,128)(2,1)S(1)} %get-tuple-element.15.own_ref), channel_id=1, source_target_pairs={{0,16},{16,0},{32,48},{48,32},{64,80},{80,64},{96,112},{112,96},{1... | collective-permute-start | bytes 294920 | tf_op jit(solution)/shard_map/ppermute | solution.py:370
  4.9 0.0 collective-permute-start
  4.9 1.4 %layout_kernel.1 = (bf16[512,256]{1,0:T(8,128)(2,1)S(1)}, bf16[96,480]{1,0:T(8,128)(2,1)S(1)}, f32[2,24,192]{2,1,0:T(8,128)S(1)}, f32[32,128]{1,0:T(8,128)S(1)},...) custom-call(bf16[9,3,32]{2,1,0:T(4,128)(2,1)} %bitcast.13, bf16[9,32,32]{2,1,0:T(8,128)(2,1)} %bitcast.12, ...), custom_call_target="tpu_custom_call" | custom-call | tf_op jit(solution)/shard_map/layout_kernel/pallas_call | solution.py:373
  6.3 0.0 collective-permute-done.1.near_ref
  6.3 2.2 %near_kernel.1 = (bf16[2,3,64,2048]{3,2,1,0:T(8,128)(2,1)S(1)}, f32[24,2048]{1,0:T(8,128)S(1)}, bf16[15,256,256]{2,1,0:T(8,128)(2,1)S(1)}) custom-call(bf16[15,256,256]{2,1,0:T(8,128)(2,1)} %constant.13.ramp_hbm, bf16[12,2,2048]{2,1,0:T(2,128)(2,1)S(1)} %get-tuple-element.15.own_ref, bf16[12,2,2048]{2,1,0:T(2,128)(2,1)S(1)} %collective-permute-done.1.near_ref, ...), custom_call_target="tpu_custom_call" | custom-call | tf_op jit(solution)/shard_map/near_kernel/pallas_call | solution.py:401
  8.5 0.1 collective-permute-done.far_ref
  8.7 2.7 %far_kernel.1 = (bf16[4,2,2048]{2,1,0:T(2,128)(2,1)}, f32[16,4,128]{2,1,0:T(4,128)S(1)}) custom-call(f32[4]{0:T(128)} %mag_hbm.1, f32[4]{0:T(128)} %move_hbm.1, f32[4]{0:T(128)} %frac_hbm.1, bf16[12,2,2048]{2,1,0:T(2,128)(2,1)S(1)} %get-tuple-element.15.own_ref, bf16[9,2,2048]{2,1,0:T(2,128)(2,1)S(1)} %collective-permute-done.far_ref, ...), custom_call_target="tpu_custom_call" | custom-call | tf_op jit(solution)/shard_map/far_kernel/pallas_call | solution.py:414
  11.3 15.8 %all_to_all.10 = f32[16,4,128]{2,1,0:T(4,128)S(1)} all-to-all(f32[16,4,128]{2,1,0:T(4,128)S(1)} %get-tuple-element.27), channel_id=1, replica_groups=mesh['ang'=16,'row'=16] {'ang'}, dimensions={0} | all-to-all | bytes 65536 | tf_op jit(solution)/shard_map/all_to_all | solution.py:435
  27.1 0.2 place_kernel.1
  27.2 16.7 %all_to_all.11 = f32[16,16,128]{2,1,0:T(8,128)S(1)} all-to-all(f32[16,16,128]{2,1,0:T(8,128)S(1)} %bitcast.10), channel_id=1, replica_groups=mesh['ang'=16,'row'=16] {'row'}, dimensions={0} | all-to-all | bytes 262144 | tf_op jit(solution)/shard_map/all_to_all | solution.py:444
  44.0 0.6 %broadcast_multiply_fusion = f32[16,128]{1,0:T(8,128)} fusion(f32[16,128]{1,0:T(8,128)S(1)} %reduce_sum.9), kind=kLoop, calls=%fused_computation | loop fusion | flops 2048 | bytes 16384 | tf_op jit(solution)/shard_map/mul | solution.py:445
  (1 shorter events, 0.0 us)
Async XLA Ops:
  1.5 4.8 %collective-permute-start.1 = (bf16[12,2,2048]{2,1,0:T(2,128)(2,1)S(1)}, bf16[12,2,2048]{2,1,0:T(2,128)(2,1)S(1)}, u32[]{:S(2)}, u32[]{:S(2)}) collective-permute-start(bf16[12,2,2048]{2,1,0:T(2,128)(2,1)S(1)} %get-tuple-element.15.own_ref), channel_id=1, source_target_pairs={{0,16},{16,0},{32,48},{48,32},{64,80},{80,64},{96,112},{112,96},{1... | collective-permute-start | bytes 294920 | tf_op jit(solution)/shard_map/ppermute | solution.py:370
  4.9 3.8 %collective-permute-start = (bf16[9,2,2048]{2,1,0:T(2,128)(2,1)S(1)}, bf16[9,2,2048]{2,1,0:T(2,128)(2,1)S(1)}, u32[]{:S(2)}, u32[]{:S(2)}) collective-permute-start(bf16[9,2,2048]{2,1,0:T(2,128)(2,1)S(1)} %get-tuple-element.16), channel_id=1, source_target_pairs={{0,240},{16,32},{32,16},{48,64},{64,48},{80,96},{96,80},{112,128},... | collective-permute-start | bytes 221192 | tf_op jit(solution)/shard_map/ppermute | solution.py:371

commit v4 on v3

--- a/solution.py
+++ b/solution.py
@@ -89,8 +89,8 @@
 
 
 def layout_kernel(
-    first_ref, middle_ref, last_ref, bias1_ref, bias2_ref, order_ref, offs_ref,
-    w1_ref, w2_ref, w3_ref, col1_ref, col2_ref, pick_ref,
+    first_ref, middle_ref, last_ref, bias1_ref, bias2_ref, order_ref, offs_ref, mag_ref, move_ref, frac_ref,
+    w1_ref, w2_ref, w3_ref, col1_ref, col2_ref, pick_ref, angle_ref,
     gather1, base2,
 ):
     f32, bf16 = jnp.float32, jnp.bfloat16
@@ -135,6 +135,11 @@
     for bias_ref, col_ref in ((bias1_ref, col1_ref), (bias2_ref, col2_ref)):
         column = jnp.sum(jnp.where(eye, jnp.broadcast_to(bias_ref[...], square), 0.0), axis=1, keepdims=True)
         col_ref[...] = jnp.broadcast_to(column, (CH, LANES))
+    ang = lax.broadcasted_iota(jnp.int32, (OUT8, ANG_DEV), 0) // ROWS_DEV
+    mine = lax.broadcasted_iota(jnp.int32, (OUT8, ANG_DEV), 1) == turned(ang, ANG_DEV - 1)
+    for at, ref in enumerate((mag_ref, move_ref, frac_ref)):
+        value = jnp.sum(jnp.where(mine, jnp.broadcast_to(ref[...], (OUT8, ANG_DEV)), 0.0), axis=1, keepdims=True)
+        angle_ref[at] = jnp.broadcast_to(value, (OUT8, LANES))
     slabs = SLABS_DEV * ROW_DEVS
     chosen = jnp.broadcast_to(order_ref[...], (slabs, slabs)) == lax.broadcasted_iota(jnp.int32, (slabs, slabs), 0)
     chosen = jnp.where(chosen, 1.0, 0.0).astype(bf16)
@@ -252,19 +257,12 @@
 
 
 def far_kernel(
-    mag_hbm, move_hbm, frac_hbm, own_ref, far_ref, shared_ref, taps_ref, ramp_ref,
+    angle_ref, own_ref, far_ref, shared_ref, taps_ref, ramp_ref,
     w1_ref, w2_ref, w3_ref, col1_ref, col2_ref,
     dual_hbm, send_ref,
-    x32, xcat, act1, act2, dual_ref, mag_ref, move_ref, frac_ref, sems,
+    x32, xcat, act1, act2, dual_ref, sem,
 ):
     f32, bf16 = jnp.float32, jnp.bfloat16
-    loads = [
-        pltpu.make_async_copy(mag_hbm, mag_ref, sems.at[0]),
-        pltpu.make_async_copy(move_hbm, move_ref, sems.at[1]),
-        pltpu.make_async_copy(frac_hbm, frac_ref, sems.at[2]),
-    ]
-    for load in loads:
-        load.start()
     bias1, bias2 = col1_ref[:, 0:1], col2_ref[:, 0:1]
     lay_inputs(x32, xcat, own_ref, far_ref, 0, HALO)
     for row in range(ROWS_DEV):
@@ -278,10 +276,8 @@
     new_dual = (own_dual + update).astype(bf16)
     for ang in range(ANG_DEV):
         dual_ref[turned(ang, ANG_DEV - 1)] = new_dual[2 * ang:2 * ang + 2, :]
-    store = pltpu.make_async_copy(dual_ref, dual_hbm, sems.at[3])
+    store = pltpu.make_async_copy(dual_ref, dual_hbm, sem)
     store.start()
-    for load in loads:
-        load.wait()
     dual32 = new_dual.astype(f32)
     blocks = jnp.concatenate([dual32[:, b * BLK:(b + 1) * BLK] for b in range(NBLK)], axis=0).astype(bf16)
     filtered = [None] * NBLK
@@ -295,15 +291,7 @@
     lanes = [filtered[t // 2][:, (t % 2) * LANES:(t % 2 + 1) * LANES] for t in range(TILES)]
     row_id = lax.broadcasted_iota(jnp.int32, (OUT8, LANES), 0)
     lane_id = lax.broadcasted_iota(jnp.int32, (OUT8, LANES), 1)
-    ang_id = row_id // ROWS_DEV
-
-    def per_angle(ref):
-        value = jnp.full((OUT8, LANES), ref[turned(0, ANG_DEV - 1)], f32)
-        for ang in range(1, ANG_DEV):
-            value = jnp.where(ang_id == ang, ref[turned(ang, ANG_DEV - 1)], value)
-        return value
-
-    mag, move, frac = per_angle(mag_ref), per_angle(move_ref), per_angle(frac_ref)
+    mag, move, frac = angle_ref[0], angle_ref[1], angle_ref[2]
     keep = 1.0 - frac
     for tile in range(TILES):
         column = (lane_id + tile * LANES).astype(f32)
@@ -370,7 +358,7 @@
     near = lax.ppermute(own, "ang", [(i, i ^ 1) for i in range(count)])
     far = lax.ppermute(far, "ang", [(i, (i + 1 if i % 2 else i - 1) % count) for i in range(count)])
     width = 3 * 4 * BLOCKS
-    w1, w2, w3, col1, col2, pick = pl.pallas_call(
+    w1, w2, w3, col1, col2, pick, angles = pl.pallas_call(
         layout_kernel,
         out_shape=(
             jax.ShapeDtypeStruct((ROWS1, 256), bf16),
@@ -379,8 +367,9 @@
             jax.ShapeDtypeStruct((CH, LANES), f32),
             jax.ShapeDtypeStruct((CH, LANES), f32),
             jax.ShapeDtypeStruct((SLABS_DEV * ROW_DEVS * SLAB_Z, width), bf16),
+            jax.ShapeDtypeStruct((3, OUT8, LANES), f32),
         ),
-        out_specs=(vmem,) * 6,
+        out_specs=(vmem,) * 7,
         scratch_shapes=[
             pltpu.VMEM((32, LANES), f32),
             pltpu.VMEM((GROUP2, 3 * GROUP1), f32),
@@ -390,7 +379,7 @@
     )(*map(in_hbm, (
         first_weight.transpose(0, 1, 3, 2).reshape(9, FIELDS, CH), middle_weight.reshape(9, CH, CH),
         last_weight.transpose(0, 2, 1, 3).reshape(3, 3, CH), first_bias[None], middle_bias[None],
-        slab_order[None], offsets,
+        slab_order[None], offsets, magnify[None], detector_shift[None], row_fraction[None],
     )))
     work = [
         pltpu.VMEM((64, U), f32),
@@ -417,21 +406,15 @@
             jax.ShapeDtypeStruct((ANG_DEV, ROWS_DEV, U), bf16),
             jax.ShapeDtypeStruct((BLOCKS, 4, LANES), f32),
         ),
-        in_specs=[hbm] * 3 + [vmem] * 10,
+        in_specs=[vmem] * 11,
         out_specs=(hbm, vmem),
         scratch_shapes=work + [
             pltpu.VMEM((ANG_DEV, ROWS_DEV, U), bf16),
-            pltpu.SMEM((ANG_DEV,), f32),
-            pltpu.SMEM((ANG_DEV,), f32),
-            pltpu.SMEM((ANG_DEV,), f32),
-            pltpu.SemaphoreType.DMA((4,)),
+            pltpu.SemaphoreType.DMA,
         ],
         compiler_params=pltpu.CompilerParams(vmem_limit_bytes=24 * MIB),
         name="far_kernel",
-    )(
-        *map(in_hbm, (magnify, detector_shift, row_fraction)),
-        own, far, shared, taps, ramp, w1, w2, w3, col1, col2,
-    )
+    )(angles, own, far, shared, taps, ramp, w1, w2, w3, col1, col2)
     got = lax.all_to_all(send, "ang", 0, 0, tiled=True)
     placed = pl.pallas_call(
         place_kernel,

time: 44.8 us -> 44.6 us (level)
  no operation moved by 1% of the time
where the time goes in v4:
time: 44.6 us; the launch traced here: 44.4 us
  blocking collectives  32.4 us (73%)
  Pallas kernels  7.18 us (16%)
  starting transfers between devices  3.33 us (7%)
  between operations  0.68 us (2%)
  other arithmetic  0.62 us (1%)
    all_to_all x1, blocking collectives, per_device(): lax.all_to_all(placed.reshape(ROW_DEVS, SLABS_DEV * SLAB_Z, LANES), 'row'...  16.7 us
    all_to_all x1, blocking collectives, per_device(): got = lax.all_to_all(send, 'ang', 0, 0, tiled=True)  15.8 us
    ppermute x1, starting transfers between devices, per_device(): near = lax.ppermute(own, 'ang', [(i, i ^ 1) for i in range(count)])  3.33 us
    pallas_call x1, Pallas kernels, per_device(): pl.pallas_call(far_kernel, out_shape=(jax.ShapeDtypeStruct((ANG_DEV, ROWS...  2.46 us
    pallas_call x1, Pallas kernels, per_device(): pl.pallas_call(near_kernel, out_shape=(jax.ShapeDtypeStruct((ROWS_DEV, 3,...  2.21 us
    pallas_call x1, Pallas kernels, per_device(): pl.pallas_call(layout_kernel, out_shape=(jax.ShapeDtypeStruct((ROWS1, 256...  1.44 us
    pallas_call x1, Pallas kernels, per_device(): pl.pallas_call(pack_kernel, out_shape=(jax.ShapeDtypeStruct((FIELDS * ANG...  0.91 us
  transfers between devices with their start and end apart: 2, of which 1 were waited for; matrix products, arithmetic and copies ran while one was open for 0% of the time, Pallas kernels for 8%

profile of v4, /device:TPU:1, one launch (start us, length us, event | category | flops | bytes accessed | tf_op | source)
XLA Modules:
  0.0 44.4 jit_solution(2077991761975139046)
XLA Ops:
  0.6 0.9 %pack_kernel.1 = (bf16[12,2,2048]{2,1,0:T(2,128)(2,1)S(1)}, bf16[9,2,2048]{2,1,0:T(2,128)(2,1)S(1)}) custom-call(bf16[4,2,2048]{2,1,0:T(2,128)(2,1)} %dual_hbm.1, bf16[4,2,2048]{2,1,0:T(2,128)(2,1)} %forw_hbm.1, bf16[4,2,2048]{2,1,0:T(2,128)(2,1)} %sino_hbm.1), custom_call_target="tpu_custom_call" | custom-call | tf_op jit(solution)/shard_map/pack_kernel/pallas_call | solution.py:345
  1.5 3.3 %collective-permute-start.1 = (bf16[12,2,2048]{2,1,0:T(2,128)(2,1)S(1)}, bf16[12,2,2048]{2,1,0:T(2,128)(2,1)S(1)}, u32[]{:S(2)}, u32[]{:S(2)}) collective-permute-start(bf16[12,2,2048]{2,1,0:T(2,128)(2,1)S(1)} %get-tuple-element.17.own_ref), channel_id=1, source_target_pairs={{0,16},{16,0},{32,48},{48,32},{64,80},{80,64},{96,112},{112,96},{1... | collective-permute-start | bytes 294920 | tf_op jit(solution)/shard_map/ppermute | solution.py:358
  4.9 0.0 collective-permute-start
  4.9 1.4 %layout_kernel.1 = (bf16[512,256]{1,0:T(8,128)(2,1)S(1)}, bf16[96,480]{1,0:T(8,128)(2,1)S(1)}, f32[2,24,192]{2,1,0:T(8,128)S(1)}, f32[32,128]{1,0:T(8,128)S(1)},...) custom-call(bf16[9,3,32]{2,1,0:T(4,128)(2,1)} %bitcast.16, ...), custom_call_target="tpu_custom_call" | custom-call | tf_op jit(solution)/shard_map/layout_kernel/pallas_call | solution.py:361
  6.3 0.0 collective-permute-done.1.near_ref
  6.3 2.2 %near_kernel.1 = (bf16[2,3,64,2048]{3,2,1,0:T(8,128)(2,1)S(1)}, f32[24,2048]{1,0:T(8,128)S(1)}, bf16[15,256,256]{2,1,0:T(8,128)(2,1)S(1)}) custom-call(bf16[15,256,256]{2,1,0:T(8,128)(2,1)} %constant.13.ramp_hbm, bf16[12,2,2048]{2,1,0:T(2,128)(2,1)S(1)} %get-tuple-element.17.own_ref, bf16[12,2,2048]{2,1,0:T(2,128)(2,1)S(1)} %collective-permute-done.1.near_ref, ...), custom_call_target="tpu_custom_call" | custom-call | tf_op jit(solution)/shard_map/near_kernel/pallas_call | solution.py:390
  8.6 0.1 collective-permute-done.far_ref
  8.7 2.5 %far_kernel.1 = (bf16[4,2,2048]{2,1,0:T(2,128)(2,1)}, f32[16,4,128]{2,1,0:T(4,128)S(1)}) custom-call(f32[3,8,128]{2,1,0:T(8,128)S(1)} %get-tuple-element.16.angle_ref, bf16[12,2,2048]{2,1,0:T(2,128)(2,1)S(1)} %get-tuple-element.17.own_ref, bf16[9,2,2048]{2,1,0:T(2,128)(2,1)S(1)} %collective-permute-done.far_ref, ...), custom_call_target="tpu_custom_call" | custom-call | tf_op jit(solution)/shard_map/far_kernel/pallas_call | solution.py:403
  11.1 15.8 %all_to_all.10 = f32[16,4,128]{2,1,0:T(4,128)S(1)} all-to-all(f32[16,4,128]{2,1,0:T(4,128)S(1)} %get-tuple-element.29), channel_id=1, replica_groups=mesh['ang'=16,'row'=16] {'ang'}, dimensions={0} | all-to-all | bytes 65536 | tf_op jit(solution)/shard_map/all_to_all | solution.py:418
  26.9 0.2 place_kernel.1
  27.1 16.7 %all_to_all.11 = f32[16,16,128]{2,1,0:T(8,128)S(1)} all-to-all(f32[16,16,128]{2,1,0:T(8,128)S(1)} %bitcast.13), channel_id=1, replica_groups=mesh['ang'=16,'row'=16] {'row'}, dimensions={0} | all-to-all | bytes 262144 | tf_op jit(solution)/shard_map/all_to_all | solution.py:427
  43.8 0.6 %broadcast_multiply_fusion = f32[16,128]{1,0:T(8,128)} fusion(f32[16,128]{1,0:T(8,128)S(1)} %reduce_sum.9), kind=kLoop, calls=%fused_computation | loop fusion | flops 2048 | bytes 16384 | tf_op jit(solution)/shard_map/mul | solution.py:428
  (1 shorter events, 0.0 us)
Async XLA Ops:
  1.5 4.8 %collective-permute-start.1 = (bf16[12,2,2048]{2,1,0:T(2,128)(2,1)S(1)}, bf16[12,2,2048]{2,1,0:T(2,128)(2,1)S(1)}, u32[]{:S(2)}, u32[]{:S(2)}) collective-permute-start(bf16[12,2,2048]{2,1,0:T(2,128)(2,1)S(1)} %get-tuple-element.17.own_ref), channel_id=1, source_target_pairs={{0,16},{16,0},{32,48},{48,32},{64,80},{80,64},{96,112},{112,96},{1... | collective-permute-start | bytes 294920 | tf_op jit(solution)/shard_map/ppermute | solution.py:358
  4.9 3.8 %collective-permute-start = (bf16[9,2,2048]{2,1,0:T(2,128)(2,1)S(1)}, bf16[9,2,2048]{2,1,0:T(2,128)(2,1)S(1)}, u32[]{:S(2)}, u32[]{:S(2)}) collective-permute-start(bf16[9,2,2048]{2,1,0:T(2,128)(2,1)S(1)} %get-tuple-element.18), channel_id=1, source_target_pairs={{0,240},{16,32},{32,16},{48,64},{64,48},{80,96},{96,80},{112,128},... | collective-permute-start | bytes 221192 | tf_op jit(solution)/shard_map/ppermute | solution.py:359

commit v5 on v4

--- a/solution.py
+++ b/solution.py
@@ -111,7 +111,7 @@
             shift = 2 * ang + row
             rolled = pltpu.roll(base1, shift, 1) if shift else base1
             start = (row * (SPAN - 2) + ang) * CH
-            w1_ref[start:start + CH, :] = rolled.astype(bf16)
+            w1_ref[start:start + CH, :] = rolled[:, 0:192].astype(bf16)
     base2[...] = jnp.zeros(base2.shape, f32)
     for ang_tap in range(3):
         for tap in range(3):
@@ -157,7 +157,7 @@
     depth = lax.broadcasted_iota(jnp.int32, (rows, width), 0) % SLAB_Z
     kind = lax.broadcasted_iota(jnp.int32, (rows, width), 1) % 4
     offset = depth + kind // 2 - kind % 2 - ROWS_DEV * lax.axis_index("row")
-    pick_ref[...] = jnp.where(starts + offset.astype(f32) == 0.0, 1.0, 0.0).astype(bf16)
+    pick_ref[...] = jnp.where(starts + offset.astype(f32) == 0.0, 0.125, 0.0).astype(bf16)
 
 
 def lay_inputs(x32, xcat, own_ref, side_ref, side, sent):
@@ -175,7 +175,6 @@
     xcat[0:64, :] = shifted(stacked, -1).astype(bf16)
     xcat[64:128, :] = stacked.astype(bf16)
     xcat[128:192, :] = shifted(stacked, 1).astype(bf16)
-    xcat[192:256, :] = jnp.zeros((64, U), bf16)
 
 
 def first_layer(xcat, w1_ref, bias1, act1, row, first, count):
@@ -361,7 +360,7 @@
     w1, w2, w3, col1, col2, pick, angles = pl.pallas_call(
         layout_kernel,
         out_shape=(
-            jax.ShapeDtypeStruct((ROWS1, 256), bf16),
+            jax.ShapeDtypeStruct((ROWS1, 192), bf16),
             jax.ShapeDtypeStruct((GROUP2, 3 * GROUP1), bf16),
             jax.ShapeDtypeStruct((2, 24, 2 * GROUP2), f32),
             jax.ShapeDtypeStruct((CH, LANES), f32),
@@ -383,7 +382,7 @@
     )))
     work = [
         pltpu.VMEM((64, U), f32),
-        pltpu.VMEM((256, U), bf16),
+        pltpu.VMEM((192, U), bf16),
         pltpu.VMEM((ROWS_DEV, 3 * GROUP1, U), bf16),
         pltpu.VMEM((ROWS_DEV * GROUP2, U), bf16),
     ]
@@ -425,7 +424,7 @@
         name="place_kernel",
     )(pick, got.reshape(4 * BLOCKS, LANES))
     shares = lax.all_to_all(placed.reshape(ROW_DEVS, SLABS_DEV * SLAB_Z, LANES), "row", 0, 0, tiled=True)
-    return new_dual, jnp.sum(shares, axis=0) * 0.125
+    return new_dual, jnp.sum(shares, axis=0)
 
 
 def solution(mesh):

time: 44.6 us -> 44.6 us (level)
    mul x1 -> x0, other arithmetic: 0.6 us -> none  [per_device(): return (new_dual, jnp.sum(shares, axis=0) * 0.125)]
    reduce_sum x1, other arithmetic: 0.02 us -> 0.62 us  [per_device(): return (new_dual, jnp.sum(shares, axis=0))]
where the time goes in v5:
time: 44.6 us; the launch traced here: 44.3 us
  blocking collectives  32.4 us (73%)
  Pallas kernels  7.15 us (16%)
  starting transfers between devices  3.33 us (7%)
  between operations  0.68 us (2%)
  other arithmetic  0.62 us (1%)
    all_to_all x1, blocking collectives, per_device(): lax.all_to_all(placed.reshape(ROW_DEVS, SLABS_DEV * SLAB_Z, LANES), 'row'...  16.7 us
    all_to_all x1, blocking collectives, per_device(): got = lax.all_to_all(send, 'ang', 0, 0, tiled=True)  15.8 us
    ppermute x1, starting transfers between devices, per_device(): near = lax.ppermute(own, 'ang', [(i, i ^ 1) for i in range(count)])  3.33 us
    pallas_call x1, Pallas kernels, per_device(): pl.pallas_call(far_kernel, out_shape=(jax.ShapeDtypeStruct((ANG_DEV, ROWS...  2.44 us
    pallas_call x1, Pallas kernels, per_device(): pl.pallas_call(near_kernel, out_shape=(jax.ShapeDtypeStruct((ROWS_DEV, 3,...  2.2 us
    pallas_call x1, Pallas kernels, per_device(): pl.pallas_call(layout_kernel, out_shape=(jax.ShapeDtypeStruct((ROWS1, 192...  1.44 us
    pallas_call x1, Pallas kernels, per_device(): pl.pallas_call(pack_kernel, out_shape=(jax.ShapeDtypeStruct((FIELDS * ANG...  0.91 us
  transfers between devices with their start and end apart: 2, of which 1 were waited for; matrix products, arithmetic and copies ran while one was open for 0% of the time, Pallas kernels for 8%

profile of v5, /device:TPU:1, one launch (start us, length us, event | category | flops | bytes accessed | tf_op | source)
XLA Modules:
  0.0 44.3 jit_solution(6375650393341332213)
XLA Ops:
  0.6 0.9 %pack_kernel.1 = (bf16[12,2,2048]{2,1,0:T(2,128)(2,1)S(1)}, bf16[9,2,2048]{2,1,0:T(2,128)(2,1)S(1)}) custom-call(bf16[4,2,2048]{2,1,0:T(2,128)(2,1)} %dual_hbm.1, bf16[4,2,2048]{2,1,0:T(2,128)(2,1)} %forw_hbm.1, bf16[4,2,2048]{2,1,0:T(2,128)(2,1)} %sino_hbm.1), custom_call_target="tpu_custom_call" | custom-call | tf_op jit(solution)/shard_map/pack_kernel/pallas_call | solution.py:344
  1.5 3.3 %collective-permute-start.1 = (bf16[12,2,2048]{2,1,0:T(2,128)(2,1)S(1)}, bf16[12,2,2048]{2,1,0:T(2,128)(2,1)S(1)}, u32[]{:S(2)}, u32[]{:S(2)}) collective-permute-start(bf16[12,2,2048]{2,1,0:T(2,128)(2,1)S(1)} %get-tuple-element.17.own_ref), channel_id=1, source_target_pairs={{0,16},{16,0},{32,48},{48,32},{64,80},{80,64},{96,112},{112,96},{1... | collective-permute-start | bytes 294920 | tf_op jit(solution)/shard_map/ppermute | solution.py:357
  4.9 0.0 collective-permute-start
  4.9 1.4 %layout_kernel.1 = (bf16[512,192]{1,0:T(8,128)(2,1)S(1)}, bf16[96,480]{1,0:T(8,128)(2,1)S(1)}, f32[2,24,192]{2,1,0:T(8,128)S(1)}, f32[32,128]{1,0:T(8,128)S(1)},...) custom-call(bf16[9,3,32]{2,1,0:T(4,128)(2,1)} %bitcast.16, ...), custom_call_target="tpu_custom_call" | custom-call | tf_op jit(solution)/shard_map/layout_kernel/pallas_call | solution.py:360
  6.3 0.0 collective-permute-done.1.near_ref
  6.3 2.2 %near_kernel.1 = (bf16[2,3,64,2048]{3,2,1,0:T(8,128)(2,1)S(1)}, f32[24,2048]{1,0:T(8,128)S(1)}, bf16[15,256,256]{2,1,0:T(8,128)(2,1)S(1)}) custom-call(bf16[15,256,256]{2,1,0:T(8,128)(2,1)} %constant.11.ramp_hbm, bf16[12,2,2048]{2,1,0:T(2,128)(2,1)S(1)} %get-tuple-element.17.own_ref, bf16[12,2,2048]{2,1,0:T(2,128)(2,1)S(1)} %collective-permute-done.1.near_ref, ...), custom_call_target="tpu_custom_call" | custom-call | tf_op jit(solution)/shard_map/near_kernel/pallas_call | solution.py:389
  8.5 0.1 collective-permute-done.far_ref
  8.7 2.4 %far_kernel.1 = (bf16[4,2,2048]{2,1,0:T(2,128)(2,1)}, f32[16,4,128]{2,1,0:T(4,128)S(1)}) custom-call(f32[3,8,128]{2,1,0:T(8,128)S(1)} %get-tuple-element.16.angle_ref, bf16[12,2,2048]{2,1,0:T(2,128)(2,1)S(1)} %get-tuple-element.17.own_ref, bf16[9,2,2048]{2,1,0:T(2,128)(2,1)S(1)} %collective-permute-done.far_ref, ...), custom_call_target="tpu_custom_call" | custom-call | tf_op jit(solution)/shard_map/far_kernel/pallas_call | solution.py:402
  11.1 15.8 %all_to_all.10 = f32[16,4,128]{2,1,0:T(4,128)S(1)} all-to-all(f32[16,4,128]{2,1,0:T(4,128)S(1)} %get-tuple-element.29), channel_id=1, replica_groups=mesh['ang'=16,'row'=16] {'ang'}, dimensions={0} | all-to-all | bytes 65536 | tf_op jit(solution)/shard_map/all_to_all | solution.py:417
  26.9 0.2 place_kernel.1
  27.0 16.7 %all_to_all.11 = f32[16,16,128]{2,1,0:T(8,128)S(1)} all-to-all(f32[16,16,128]{2,1,0:T(8,128)S(1)} %bitcast.13), channel_id=1, replica_groups=mesh['ang'=16,'row'=16] {'row'}, dimensions={0} | all-to-all | bytes 262144 | tf_op jit(solution)/shard_map/all_to_all | solution.py:426
  43.7 0.6 %reduce_sum.9 = f32[16,128]{1,0:T(8,128)} reduce(f32[16,16,128]{2,1,0:T(8,128)S(1)} %all_to_all.11, f32[]{:T(128)} %constant.1.clone.1), dimensions={0}, to_apply=%region_0.0 | reduce | flops 30720 | bytes 139268 | tf_op jit(solution)/shard_map/reduce_sum | solution.py:427
Async XLA Ops:
  1.5 4.8 %collective-permute-start.1 = (bf16[12,2,2048]{2,1,0:T(2,128)(2,1)S(1)}, bf16[12,2,2048]{2,1,0:T(2,128)(2,1)S(1)}, u32[]{:S(2)}, u32[]{:S(2)}) collective-permute-start(bf16[12,2,2048]{2,1,0:T(2,128)(2,1)S(1)} %get-tuple-element.17.own_ref), channel_id=1, source_target_pairs={{0,16},{16,0},{32,48},{48,32},{64,80},{80,64},{96,112},{112,96},{1... | collective-permute-start | bytes 294920 | tf_op jit(solution)/shard_map/ppermute | solution.py:357
  4.9 3.8 %collective-permute-start = (bf16[9,2,2048]{2,1,0:T(2,128)(2,1)S(1)}, bf16[9,2,2048]{2,1,0:T(2,128)(2,1)S(1)}, u32[]{:S(2)}, u32[]{:S(2)}) collective-permute-start(bf16[9,2,2048]{2,1,0:T(2,128)(2,1)S(1)} %get-tuple-element.18), channel_id=1, source_target_pairs={{0,240},{16,32},{32,16},{48,64},{64,48},{80,96},{96,80},{112,128},... | collective-permute-start | bytes 221192 | tf_op jit(solution)/shard_map/ppermute | solution.py:358

commit v6 on v5

--- a/solution.py
+++ b/solution.py
@@ -76,12 +76,10 @@
     return index + parity() * (last - 2 * index)
 
 
-def pack_kernel(dual_hbm, forw_hbm, sino_hbm, own_ref, far_ref, sems):
+def pack_kernel(dual_hbm, forw_hbm, sino_hbm, own_ref, sems):
     loads = []
     for at, field in enumerate((dual_hbm, forw_hbm, sino_hbm)):
-        side = field.at[pl.ds(parity(), HALO)]
-        loads.append(pltpu.make_async_copy(side, far_ref.at[pl.ds(at * HALO, HALO)], sems.at[at]))
-        loads.append(pltpu.make_async_copy(field, own_ref.at[pl.ds(at * ANG_DEV, ANG_DEV)], sems.at[3 + at]))
+        loads.append(pltpu.make_async_copy(field, own_ref.at[pl.ds(at * ANG_DEV, ANG_DEV)], sems.at[at]))
     for load in loads:
         load.start()
     for load in loads:
@@ -160,7 +158,7 @@
     pick_ref[...] = jnp.where(starts + offset.astype(f32) == 0.0, 0.125, 0.0).astype(bf16)
 
 
-def lay_inputs(x32, xcat, own_ref, side_ref, side, sent):
+def lay_inputs(x32, xcat, own_ref, side_ref, side, skip):
     f32, bf16 = jnp.float32, jnp.bfloat16
     x32[...] = jnp.zeros(x32.shape, f32)
     for field in range(FIELDS):
@@ -170,7 +168,7 @@
             x32[at:at + 2, :] = own_ref[field * ANG_DEV + turned(ang, ANG_DEV - 1)].astype(f32)
         for ang in range(HALO):
             at = base + 2 * (side + ang)
-            x32[at:at + 2, :] = side_ref[field * sent + turned(ang, sent - 1)].astype(f32)
+            x32[at:at + 2, :] = side_ref[field * ANG_DEV + turned(skip + ang, ANG_DEV - 1)].astype(f32)
     stacked = x32[...]
     xcat[0:64, :] = shifted(stacked, -1).astype(bf16)
     xcat[64:128, :] = stacked.astype(bf16)
@@ -245,7 +243,7 @@
     load = pltpu.make_async_copy(ramp_hbm, ramp_ref, sem)
     load.start()
     bias1, bias2 = col1_ref[:, 0:1], col2_ref[:, 0:1]
-    lay_inputs(x32, xcat, own_ref, near_ref, HALO + ANG_DEV, ANG_DEV)
+    lay_inputs(x32, xcat, own_ref, near_ref, HALO + ANG_DEV, 0)
     for row in range(ROWS_DEV):
         first_layer_whole(xcat, w1_ref, bias1, act1, row, 3, 5)
         for tap in range(3):
@@ -263,7 +261,7 @@
 ):
     f32, bf16 = jnp.float32, jnp.bfloat16
     bias1, bias2 = col1_ref[:, 0:1], col2_ref[:, 0:1]
-    lay_inputs(x32, xcat, own_ref, far_ref, 0, HALO)
+    lay_inputs(x32, xcat, own_ref, far_ref, 0, 1)
     for row in range(ROWS_DEV):
         first_layer(xcat, w1_ref, bias1, act1, row, 0, 3)
         for tap in range(3):
@@ -341,21 +339,18 @@
     f32, bf16 = jnp.float32, jnp.bfloat16
     vmem = pl.BlockSpec(memory_space=pltpu.VMEM)
     hbm = pl.BlockSpec(memory_space=pltpu.HBM)
-    own, far = pl.pallas_call(
+    own = pl.pallas_call(
         pack_kernel,
-        out_shape=(
-            jax.ShapeDtypeStruct((FIELDS * ANG_DEV, ROWS_DEV, U), bf16),
-            jax.ShapeDtypeStruct((FIELDS * HALO, ROWS_DEV, U), bf16),
-        ),
+        out_shape=jax.ShapeDtypeStruct((FIELDS * ANG_DEV, ROWS_DEV, U), bf16),
         in_specs=[hbm] * 3,
-        out_specs=(vmem,) * 2,
-        scratch_shapes=[pltpu.SemaphoreType.DMA((6,))],
+        out_specs=vmem,
+        scratch_shapes=[pltpu.SemaphoreType.DMA((3,))],
         compiler_params=pltpu.CompilerParams(vmem_limit_bytes=2 * MIB),
         name="pack_kernel",
     )(*map(in_hbm, (dual_field, forward, sinogram)))
     count = lax.axis_size("ang")
     near = lax.ppermute(own, "ang", [(i, i ^ 1) for i in range(count)])
-    far = lax.ppermute(far, "ang", [(i, (i + 1 if i % 2 else i - 1) % count) for i in range(count)])
+    far = lax.ppermute(own, "ang", [(i, (i + 1 if i % 2 else i - 1) % count) for i in range(count)])
     width = 3 * 4 * BLOCKS
     w1, w2, w3, col1, col2, pick, angles = pl.pallas_call(
         layout_kernel,

time: 44.6 us -> 44.8 us (level)
  no operation moved by 1% of the time
where the time goes in v6:
time: 44.8 us; the launch traced here: 44.5 us
  blocking collectives  32.4 us (72%)
  Pallas kernels  7.06 us (16%)
  starting transfers between devices  3.33 us (7%)
  between operations  0.68 us (2%)
  other arithmetic  0.62 us (1%)
    all_to_all x1, blocking collectives, per_device(): lax.all_to_all(placed.reshape(ROW_DEVS, SLABS_DEV * SLAB_Z, LANES), 'row'...  16.7 us
    all_to_all x1, blocking collectives, per_device(): got = lax.all_to_all(send, 'ang', 0, 0, tiled=True)  15.8 us
    ppermute x1, starting transfers between devices, per_device(): near = lax.ppermute(own, 'ang', [(i, i ^ 1) for i in range(count)])  3.33 us
    pallas_call x1, Pallas kernels, per_device(): pl.pallas_call(far_kernel, out_shape=(jax.ShapeDtypeStruct((ANG_DEV, ROWS...  2.45 us
    pallas_call x1, Pallas kernels, per_device(): pl.pallas_call(near_kernel, out_shape=(jax.ShapeDtypeStruct((ROWS_DEV, 3,...  2.2 us
    pallas_call x1, Pallas kernels, per_device(): pl.pallas_call(layout_kernel, out_shape=(jax.ShapeDtypeStruct((ROWS1, 192...  1.44 us
  transfers between devices with their start and end apart: 2, of which 1 were waited for; matrix products, arithmetic and copies ran while one was open for 0% of the time, Pallas kernels for 8%

profile of v6, /device:TPU:1, one launch (start us, length us, event | category | flops | bytes accessed | tf_op | source)
XLA Modules:
  0.0 44.5 jit_solution(12487313589585314021)
XLA Ops:
  0.6 0.8 %pack_kernel.1.own_ref = bf16[12,2,2048]{2,1,0:T(2,128)(2,1)S(1)} custom-call(bf16[4,2,2048]{2,1,0:T(2,128)(2,1)} %dual_hbm.1, bf16[4,2,2048]{2,1,0:T(2,128)(2,1)} %forw_hbm.1, bf16[4,2,2048]{2,1,0:T(2,128)(2,1)} %sino_hbm.1), custom_call_target="tpu_custom_call" | custom-call | tf_op jit(solution)/shard_map/pack_kernel/pallas_call | solution.py:342
  1.5 3.3 %collective-permute-start.1 = (bf16[12,2,2048]{2,1,0:T(2,128)(2,1)S(1)}, bf16[12,2,2048]{2,1,0:T(2,128)(2,1)S(1)}, u32[]{:S(2)}, u32[]{:S(2)}) collective-permute-start(bf16[12,2,2048]{2,1,0:T(2,128)(2,1)S(1)} %pack_kernel.1.own_ref), channel_id=1, source_target_pairs={{0,16},{16,0},{32,48},{48,32},{64,80},{80,64},{96,112},{112,96},{1... | collective-permute-start | bytes 294920 | tf_op jit(solution)/shard_map/ppermute | solution.py:352
  4.8 0.0 collective-permute-start
  4.8 1.4 %layout_kernel.1 = (bf16[512,192]{1,0:T(8,128)(2,1)S(1)}, bf16[96,480]{1,0:T(8,128)(2,1)S(1)}, f32[2,24,192]{2,1,0:T(8,128)S(1)}, f32[32,128]{1,0:T(8,128)S(1)},...) custom-call(bf16[9,3,32]{2,1,0:T(4,128)(2,1)} %bitcast.16, ...), custom_call_target="tpu_custom_call" | custom-call | tf_op jit(solution)/shard_map/layout_kernel/pallas_call | solution.py:355
  6.2 0.0 collective-permute-done.1.near_ref
  6.2 2.2 %near_kernel.1 = (bf16[2,3,64,2048]{3,2,1,0:T(8,128)(2,1)S(1)}, f32[24,2048]{1,0:T(8,128)S(1)}, bf16[15,256,256]{2,1,0:T(8,128)(2,1)S(1)}) custom-call(bf16[15,256,256]{2,1,0:T(8,128)(2,1)} %constant.11.ramp_hbm, bf16[12,2,2048]{2,1,0:T(2,128)(2,1)S(1)} %pack_kernel.1.own_ref, bf16[12,2,2048]{2,1,0:T(2,128)(2,1)S(1)} %collective-permute-done.1.near_ref, ...), custom_call_target="tpu_custom_call" | custom-call | tf_op jit(solution)/shard_map/near_kernel/pallas_call | solution.py:384
  8.4 0.4 collective-permute-done.far_ref
  8.8 2.4 %far_kernel.1 = (bf16[4,2,2048]{2,1,0:T(2,128)(2,1)}, f32[16,4,128]{2,1,0:T(4,128)S(1)}) custom-call(f32[3,8,128]{2,1,0:T(8,128)S(1)} %get-tuple-element.14.angle_ref, bf16[12,2,2048]{2,1,0:T(2,128)(2,1)S(1)} %pack_kernel.1.own_ref, bf16[12,2,2048]{2,1,0:T(2,128)(2,1)S(1)} %collective-permute-done.far_ref, ...), custom_call_target="tpu_custom_call" | custom-call | tf_op jit(solution)/shard_map/far_kernel/pallas_call | solution.py:397
  11.3 15.8 %all_to_all.10 = f32[16,4,128]{2,1,0:T(4,128)S(1)} all-to-all(f32[16,4,128]{2,1,0:T(4,128)S(1)} %get-tuple-element.25), channel_id=1, replica_groups=mesh['ang'=16,'row'=16] {'ang'}, dimensions={0} | all-to-all | bytes 65536 | tf_op jit(solution)/shard_map/all_to_all | solution.py:412
  27.1 0.2 place_kernel.1
  27.2 16.7 %all_to_all.11 = f32[16,16,128]{2,1,0:T(8,128)S(1)} all-to-all(f32[16,16,128]{2,1,0:T(8,128)S(1)} %bitcast.13), channel_id=1, replica_groups=mesh['ang'=16,'row'=16] {'row'}, dimensions={0} | all-to-all | bytes 262144 | tf_op jit(solution)/shard_map/all_to_all | solution.py:421
  43.9 0.6 %reduce_sum.9 = f32[16,128]{1,0:T(8,128)} reduce(f32[16,16,128]{2,1,0:T(8,128)S(1)} %all_to_all.11, f32[]{:T(128)} %constant.1.clone.1), dimensions={0}, to_apply=%region_0.0 | reduce | flops 30720 | bytes 139268 | tf_op jit(solution)/shard_map/reduce_sum | solution.py:422
Async XLA Ops:
  1.5 4.8 %collective-permute-start.1 = (bf16[12,2,2048]{2,1,0:T(2,128)(2,1)S(1)}, bf16[12,2,2048]{2,1,0:T(2,128)(2,1)S(1)}, u32[]{:S(2)}, u32[]{:S(2)}) collective-permute-start(bf16[12,2,2048]{2,1,0:T(2,128)(2,1)S(1)} %pack_kernel.1.own_ref), channel_id=1, source_target_pairs={{0,16},{16,0},{32,48},{48,32},{64,80},{80,64},{96,112},{112,96},{1... | collective-permute-start | bytes 294920 | tf_op jit(solution)/shard_map/ppermute | solution.py:352
  4.8 4.0 %collective-permute-start = (bf16[12,2,2048]{2,1,0:T(2,128)(2,1)S(1)}, bf16[12,2,2048]{2,1,0:T(2,128)(2,1)S(1)}, u32[]{:S(2)}, u32[]{:S(2)}) collective-permute-start(bf16[12,2,2048]{2,1,0:T(2,128)(2,1)S(1)} %pack_kernel.1.own_ref), channel_id=1, source_target_pairs={{0,240},{16,32},{32,16},{48,64},{64,48},{80,96},{96,80},{112,128},... | collective-permute-start | bytes 294920 | tf_op jit(solution)/shard_map/ppermute | solution.py:353
